TPU v7x, 128 devices: a whole 4x4x4 slice. The times are simulated.
128 devices in a mesh: seq: 16 (over y, z_hi, core), head: 8 (over x, z_lo).
Axes of the slice: x: 4, y: 4, z: 4 (z_hi: 2, z_lo: 2; z = z_hi * 2 + z_lo), core: 2. Of those that a mesh axis runs over, the one named last changes fastest.
Arguments:
- teacher_queries: bfloat16 [4096, 8192], P('seq', 'head'), may hold values from -16 to 16, as said below
- student_queries: bfloat16 [4096, 4096], P('seq', 'head'), may hold values from -16 to 16, as said below
- token_counts: int32 [16], replicated, may hold values from 1 to 256, 3072 in all
Outputs:
- student_grad: float32 [4096, 4096], P('seq', 'head')
- loss: float32 [], replicated
Inputs may be any that keep to these rules, and one draw needn't show every extreme that they name: `teacher_queries`: query entries are real values of order one; the entries of a row may share a scale. `student_queries`: query entries are real values of order one; the entries of a row may share a scale. `token_counts`: the counts sum to 3072; the largest equals 256.
All inputs are finite; a program needn't handle non-finite values.
Results may differ from a plain program's by a relative error of at most 0.0035.
Values may be sent and summed in bfloat16 or wider, within the bound.
A program may use at most 64 MiB of HBM per device.

v0:
```python
import jax
import jax.numpy as jnp
from jax import lax
from jax.sharding import Mesh
from jax.sharding import PartitionSpec as P

DT = 8192
DS = 4096
H_REL = 128
HEAD = ("head_0", "head_1")
SEQ = ("seq_0", "seq_1", "seq_2")
SEQ_HEAD = ("seq_0", "seq_1", "seq_2", "head_0", "head_1")


NEGATIVE = -1e30


def in_one_piece(arrays, axis, dim, along):
    widths = [a.shape[along] for a in arrays]
    both = jnp.concatenate(arrays, axis=along)
    filled = lax.all_gather(both, axis, axis=dim, tiled=True)
    return tuple(jnp.split(filled, [sum(widths[:k]) for k in range(1, len(widths))], axis=along))


def one_axis_at_a_time(shard, axes):
    for axis in axes:
        shard = lax.psum(shard, axis)
    return shard


def in_order(pieces, dim):
    dims = list(pieces.shape[1:])
    dims[dim] *= pieces.shape[0]
    return jnp.moveaxis(pieces, 0, dim).reshape(dims)


def sent_to_all(shard, axis):
    size = lax.axis_size(axis)
    return lax.all_to_all(
        jnp.broadcast_to(shard[None], (size, *shard.shape)), axis, 0, 0, tiled=True
    )


def gather_directly(shard, axis, dim):
    return in_order(sent_to_all(shard, axis), dim)


def tile_logits(query_set, key_set, scales):
    teacher_logits = (
        jnp.einsum("rhd,khd->hrk", query_set[0], key_set[0], preferred_element_type=jnp.float32)
        * scales[0]
    )
    student_logits = (
        jnp.einsum("rhd,khd->hrk", query_set[1], key_set[1], preferred_element_type=jnp.float32)
        * scales[1]
    )
    row_pos = query_set[2]
    key_pos = key_set[2]
    allowed = (key_pos[None, :] <= row_pos[:, None]) & (
        key_set[3][None, :] | (key_pos[None, :] == row_pos[:, None])
    )
    return (teacher_logits, student_logits, allowed[None])


def grad_weights(query_set, stats, key_set, scales):
    teacher_logits, student_logits, allowed = tile_logits(query_set, key_set, scales)
    teacher_prob = (
        jnp.where(allowed, jnp.exp(teacher_logits - stats[0][..., None]), 0.0) / stats[1][..., None]
    )
    student_prob = (
        jnp.where(allowed, jnp.exp(student_logits - stats[2][..., None]), 0.0) / stats[3][..., None]
    )
    difference = jnp.where(query_set[3][None, :, None], student_prob - teacher_prob, 0.0)
    return difference.astype(jnp.bfloat16)


def row_statistics(query_set, halves, half_rows, select, scales):
    row_count = query_set[0].shape[0]
    heads_here = query_set[0].shape[1]
    lowest = jnp.full((heads_here, row_count), NEGATIVE, jnp.float32)
    zeros = jnp.zeros((heads_here, row_count), jnp.float32)

    def advance(index_now, loop_state):
        teacher_max, teacher_sum, cross_sum, student_max, student_sum = loop_state
        key_set = select(index_now * half_rows, half_rows)
        teacher_logits, student_logits, allowed = tile_logits(query_set, key_set, scales)
        teacher_top = jnp.maximum(
            teacher_max, jnp.max(jnp.where(allowed, teacher_logits, NEGATIVE), axis=2)
        )
        student_top = jnp.maximum(
            student_max, jnp.max(jnp.where(allowed, student_logits, NEGATIVE), axis=2)
        )
        teacher_weight = jnp.where(allowed, jnp.exp(teacher_logits - teacher_top[..., None]), 0.0)
        student_weight = jnp.where(allowed, jnp.exp(student_logits - student_top[..., None]), 0.0)
        teacher_shrink = jnp.exp(teacher_max - teacher_top)
        student_shrink = jnp.exp(student_max - student_top)
        teacher_sum = teacher_sum * teacher_shrink + jnp.sum(teacher_weight, axis=2)
        cross_sum = cross_sum * teacher_shrink + jnp.sum(
            teacher_weight * (teacher_logits - student_logits), axis=2
        )
        student_sum = student_sum * student_shrink + jnp.sum(student_weight, axis=2)
        return (teacher_top, teacher_sum, cross_sum, student_top, student_sum)

    teacher_max, teacher_sum, cross_sum, student_max, student_sum = lax.fori_loop(
        0, halves, advance, (lowest, zeros, zeros, lowest, zeros)
    )
    divergence = (
        cross_sum / teacher_sum
        - teacher_max
        - jnp.log(teacher_sum)
        + student_max
        + jnp.log(student_sum)
    )
    divergence_sum = jnp.sum(jnp.where(query_set[3][None, :], divergence, 0.0))
    return ((teacher_max, teacher_sum, student_max, student_sum), divergence_sum)


def local(teacher_queries, student_queries, token_counts):
    block_rows = teacher_queries.shape[0]
    half_rows = block_rows // 2
    heads_here = H_REL // lax.axis_size(HEAD)
    teacher_dim = DT // H_REL
    student_dim = DS // H_REL
    scales = (teacher_dim ** (-0.5), student_dim ** (-0.5))
    blocks = lax.axis_size(SEQ)
    my_index = lax.axis_index(SEQ)
    seq_rows = block_rows * blocks
    teacher_all, student_all = in_one_piece((teacher_queries, student_queries), SEQ, 0, 1)
    teacher_all = teacher_all.reshape(seq_rows, heads_here, teacher_dim)
    student_all = student_all.reshape(seq_rows, heads_here, student_dim)
    positions = jnp.arange(seq_rows, dtype=jnp.int32)
    owner_table = (positions // block_rows)[:, None] == jnp.arange(blocks, dtype=jnp.int32)[None, :]
    real_count = jnp.sum(jnp.where(owner_table, token_counts[None, :], 0), axis=1)
    is_real = positions % block_rows < real_count

    def select(row_start, row_count):
        return (
            lax.dynamic_slice_in_dim(teacher_all, row_start, row_count, 0),
            lax.dynamic_slice_in_dim(student_all, row_start, row_count, 0),
            lax.dynamic_slice_in_dim(positions, row_start, row_count, 0),
            lax.dynamic_slice_in_dim(is_real, row_start, row_count, 0),
        )

    groups = [
        (my_index * half_rows, half_rows, my_index + 1),
        ((2 * blocks - 1 - my_index) * half_rows, half_rows, 2 * blocks - my_index),
    ]
    group_stats = []
    divergence_sum = jnp.zeros((), jnp.float32)
    for row_start, row_count, halves in groups:
        stats, group_sum = row_statistics(
            select(row_start, row_count), halves, half_rows, select, scales
        )
        group_stats.append(stats)
        divergence_sum = divergence_sum + group_sum
    loss = one_axis_at_a_time(divergence_sum, SEQ_HEAD) / (
        H_REL * jnp.sum(token_counts).astype(jnp.float32)
    )
    local_stats = tuple(
        (jnp.concatenate([stats[member] for stats in group_stats], axis=1) for member in range(4))
    )
    full_stats = jax.tree.map(lambda part: gather_directly(part, SEQ, 1), local_stats)
    reordered = []
    for member in full_stats:
        folded = member.reshape(heads_here, blocks, 2, half_rows)
        lower_part = folded[:, :, 0].reshape(heads_here, blocks * half_rows)
        upper_part = folded[:, ::-1, 1].reshape(heads_here, blocks * half_rows)
        reordered.append(jnp.concatenate([lower_part, upper_part], axis=1))
    full_stats = tuple(reordered)
    own_start = my_index * block_rows
    own_set = select(own_start, block_rows)
    own_stats = tuple(
        (lax.dynamic_slice_in_dim(member, own_start, block_rows, 1) for member in full_stats)
    )

    def query_side(index_now, query_grad):
        key_set = select(index_now * half_rows, half_rows)
        weights = grad_weights(own_set, own_stats, key_set, scales)
        return query_grad + jnp.einsum(
            "hrk,khd->rhd", weights, key_set[1], preferred_element_type=jnp.float32
        )

    def key_side(index_now, key_grad):
        query_start = index_now * half_rows
        query_set = select(query_start, half_rows)
        query_stats = tuple(
            (lax.dynamic_slice_in_dim(member, query_start, half_rows, 1) for member in full_stats)
        )
        weights = grad_weights(query_set, query_stats, own_set, scales)
        return key_grad + jnp.einsum(
            "hrk,rhd->khd", weights, query_set[1], preferred_element_type=jnp.float32
        )

    empty = jnp.zeros((block_rows, heads_here, student_dim), jnp.float32)
    query_grad = lax.fori_loop(0, 2 * my_index + 2, query_side, empty)
    key_grad = lax.fori_loop(2 * my_index, 2 * blocks, key_side, empty)
    student_grad = ((query_grad + key_grad) * scales[1]).reshape(
        block_rows, heads_here * student_dim
    )
    return (student_grad, loss)


def solution(mesh):
    finer = Mesh(
        mesh.devices.reshape(4, 2, 2, 4, 2), ("seq_0", "seq_1", "seq_2", "head_0", "head_1")
    )
    return jax.shard_map(
        local,
        mesh=finer,
        in_specs=(P(SEQ, HEAD), P(SEQ, HEAD), P()),
        out_specs=(P(SEQ, HEAD), P()),
        check_vma=False,
    )
```

profile of v0, /device:TPU:1, one launch (start us, length us, event | category | flops | bytes accessed | tf_op | source)
XLA Modules:
  0.0 549.3 jit_solution(9238639614915139021)
XLA Ops:
  13.4 101.6 %all-gather.2.cloned.1.call-done = bf16[4096,1536]{0,1:T(8,128)(2,1)} async-done(((bf16[256,1536]{0,1:T(8,128)(2,1)}), bf16[4096,1536]{0,1:T(8,128)(2,1)}) %all-gather.2.cloned.1.call-update) | async-done | bytes 12582928 | tf_op jit(solution)/shard_map/all_gather | solution.py:21
  115.0 7.7 %split.9 = bf16[4096,1024]{0,1:T(8,128)(2,1)} slice(bf16[4096,1536]{0,1:T(8,128)(2,1)} %all-gather.2.cloned.1.call-done), slice={[0:4096], [0:1024]} | slice | bytes 16777216 | tf_op jit(solution)/shard_map/split | solution.py:22
  123.8 2.5 split.8
  126.4 1.8 copy-done
  128.2 7.1 %while.56 = (s32[]{:T(128)}, f32[16,128]{1,0:T(8,128)S(1)}, f32[16,128]{1,0:T(8,128)S(1)}, f32[16,128]{1,0:T(8,128)S(1)}, f32[16,128]{1,0:T(8,128)S(1)}, /*index...) while((s32[]{:T(128)}, f32[16,128]{1,0:T(8,128)S(1)}, ...), condition=%wide.region_7.8_spmd, body=%wide.region_1.7_spmd.sunk | while | flops 54339588 | bytes 6326883 | solution.py:104
  135.4 111.2 %while.57 = (s32[]{:T(128)}, f32[16,128]{1,0:T(8,128)S(1)}, f32[16,128]{1,0:T(8,128)S(1)}, f32[16,128]{1,0:T(8,128)S(1)}, f32[16,128]{1,0:T(8,128)S(1)}, /*index...) while((s32[]{:T(128)}, f32[16,128]{1,0:T(8,128)S(1)}, ...), condition=%wide.region_14.15_spmd, body=%wide.region_8.14_spmd.sunk | while | flops 54339588 | bytes 6326883 | solution.py:104
  248.6 8.1 %psum.35 = f32[]{:T(128)} all-reduce(f32[]{:T(128)S(6)} %add.150), channel_id=1, replica_groups=mesh['seq_0'=4,'seq_1'=2,'seq_2'=2,'head_0'=4,'head_1'=2] {'seq_0'}, use_global_device_ids=true, to_apply=%region_21.22 | all-reduce | flops 1 | bytes 8 | tf_op jit(solution)/shard_map/psum | solution.py:27
  256.6 5.9 %psum.36 = f32[]{:T(128)} all-reduce(f32[]{:T(128)} %psum.35), channel_id=1, replica_groups=mesh['seq_0'=4,'seq_1'=2,'seq_2'=2,'head_0'=4,'head_1'=2] {'seq_1'}, use_global_device_ids=true, to_apply=%region_22.23 | all-reduce | flops 1 | bytes 8 | tf_op jit(solution)/shard_map/psum | solution.py:27
  262.5 6.2 %psum.37 = f32[]{:T(128)} all-reduce(f32[]{:T(128)} %psum.36), channel_id=1, replica_groups=mesh['seq_0'=4,'seq_1'=2,'seq_2'=2,'head_0'=4,'head_1'=2] {'seq_2'}, use_global_device_ids=true, to_apply=%region_23.24 | all-reduce | flops 1 | bytes 8 | tf_op jit(solution)/shard_map/psum | solution.py:27
  268.7 9.0 %psum.38 = f32[]{:T(128)} all-reduce(f32[]{:T(128)} %psum.37), channel_id=1, replica_groups=mesh['seq_0'=4,'seq_1'=2,'seq_2'=2,'head_0'=4,'head_1'=2] {'head_0'}, use_global_device_ids=true, to_apply=%region_24.25 | all-reduce | flops 1 | bytes 8 | tf_op jit(solution)/shard_map/psum | solution.py:27
  278.4 5.7 %all-to-all-start.2 = ((f32[16,16,256]{2,1,0:T(8,128)}), f32[16,16,256]{2,1,0:T(8,128)S(1)}, u32[]{:S(2)}, u32[]{:S(2)}) async-start(f32[16,16,256]{2,1,0:T(8,128)} %broadcast_in_dim.203), calls=%async_computation.2 | async-start | bytes 524288 | tf_op jit(solution)/shard_map/all_to_all | solution.py:39
  284.1 4.7 psum.39
  290.5 1.9 constant_dynamic-slice_fusion.6
  293.8 7.6 %all-to-all-start.3 = ((f32[16,16,256]{2,1,0:T(8,128)}), f32[16,16,256]{2,1,0:T(8,128)S(1)}, u32[]{:S(2)}, u32[]{:S(2)}) async-start(f32[16,16,256]{2,1,0:T(8,128)} %broadcast_in_dim.204), calls=%async_computation.3 | async-start | bytes 524288 | tf_op jit(solution)/shard_map/all_to_all | solution.py:39
  302.2 8.1 %all-to-all-done.3 = f32[16,16,256]{2,1,0:T(8,128)S(1)} async-done(((f32[16,16,256]{2,1,0:T(8,128)}), f32[16,16,256]{2,1,0:T(8,128)S(1)}, u32[]{:S(2)}, u32[]{:S(2)}) %all-to-all-start.3) | async-done | bytes 262176 | tf_op jit(solution)/shard_map/all_to_all | solution.py:39
  311.0 3.7 all-to-all-start
  315.5 8.1 %all-to-all-done = f32[16,16,256]{2,1,0:T(8,128)S(1)} async-done(((f32[16,16,256]{2,1,0:T(8,128)}), f32[16,16,256]{2,1,0:T(8,128)S(1)}, u32[]{:S(2)}, u32[]{:S(2)}) %all-to-all-start) | async-done | bytes 262176 | tf_op jit(solution)/shard_map/all_to_all | solution.py:39
  324.3 3.7 all-to-all-start.1
  329.5 7.5 %all-to-all-done.1 = f32[16,16,256]{2,1,0:T(8,128)S(1)} async-done(((f32[16,16,256]{2,1,0:T(8,128)}), f32[16,16,256]{2,1,0:T(8,128)S(1)}, u32[]{:S(2)}, u32[]{:S(2)}) %all-to-all-start.1) | async-done | bytes 262176 | tf_op jit(solution)/shard_map/all_to_all | solution.py:39
  340.1 179.9 %while.59 = (s32[]{:T(128)}, f32[256,16,32]{0,2,1:T(8,128)S(1)}, bf16[4096,16,32]{0,2,1:T(8,128)(2,1)}, pred[4096]{0:T(1024)(128)(4,1)}, s32[256]{0:T(256)S(1)},...) while((s32[]{:T(128)}, f32[256,16,32]{0,2,1:T(8,128)S(1)}, ...), condition=%wide.region_18.19_spmd, body=%wide.region_17.18_spmd.sunk | while | flops 140247040 | bytes 6721895 | solution.py:196
  343.2 2.9 fusion.127
  349.2 2.9 fusion.127
  352.1 1.4 fusion.126
  355.2 2.9 fusion.127
  361.2 2.9 fusion.127
  367.2 2.9 fusion.127
  373.2 2.9 fusion.127
  376.1 1.4 fusion.126
  379.2 2.9 fusion.127
  385.2 2.9 fusion.127
  391.1 2.9 fusion.127
  394.1 1.4 fusion.126
  397.1 2.9 fusion.127
  403.1 2.9 fusion.127
  409.1 2.9 fusion.127
  415.1 2.9 fusion.127
  418.0 1.4 fusion.126
  421.1 2.9 fusion.127
  427.1 2.9 fusion.127
  433.1 2.9 fusion.127
  439.1 2.9 fusion.127
  445.1 2.9 fusion.127
  448.0 1.4 fusion.126
  451.1 2.9 fusion.127
  457.1 2.9 fusion.127
  463.1 2.9 fusion.127
  469.1 2.9 fusion.127
  475.1 2.9 fusion.127
  481.1 2.9 fusion.127
  487.1 2.9 fusion.127
  493.1 2.9 fusion.127
  499.2 2.9 fusion.127
  505.2 2.9 fusion.127
  511.2 2.9 fusion.127
  517.2 2.9 fusion.127
  520.1 20.1 %while.58 = (s32[]{:T(128)}, f32[256,16,32]{0,2,1:T(8,128)S(1)}, s32[]{:T(128)}, bf16[4096,16,32]{0,2,1:T(8,128)(2,1)}, pred[256]{0:T(512)(128)(4,1)S(1)}, /*ind...) while((s32[]{:T(128)}, f32[256,16,32]{0,2,1:T(8,128)S(1)}, ...), condition=%wide.region_16.17_spmd, body=%wide.region_15.16_spmd.sunk | while | flops 140247040 | bytes 6754691 | solution.py:195
  521.1 1.4 fusion.119
  522.5 2.6 fusion.120
  526.1 1.4 fusion.119
  527.5 2.6 fusion.120
  531.1 1.4 fusion.119
  532.6 2.6 fusion.120
  536.2 1.4 fusion.119
  537.6 2.6 fusion.120
  (640 shorter events, 223.0 us)
Async XLA Ops:
  7.2 3.4 copy-start.6
  7.2 107.9 %all-gather.2.cloned.1.call-start = ((), (), s32[]{:S(2)}) async-start(), calls=%async_computation.4 | async-start | bytes 13369344 | tf_op jit(solution)/shard_map/all_gather | solution.py:21
  126.3 1.9 copy-start
  246.6 31.8 %copy-start.5 = (pred[4096]{0:T(1024)(128)(4,1)}, pred[4096]{0:T(1024)(128)(4,1)S(1)}, u32[]{:S(2)}) copy-start(pred[4096]{0:T(1024)(128)(4,1)S(1)} %get-tuple-element.1167) | copy-start | bytes 12292
  278.4 14.6 %all-to-all-start.2 = ((f32[16,16,256]{2,1,0:T(8,128)}), f32[16,16,256]{2,1,0:T(8,128)S(1)}, u32[]{:S(2)}, u32[]{:S(2)}) async-start(f32[16,16,256]{2,1,0:T(8,128)} %broadcast_in_dim.203), calls=%async_computation.2 | async-start | bytes 524288 | tf_op jit(solution)/shard_map/all_to_all | solution.py:39
  293.8 16.5 %all-to-all-start.3 = ((f32[16,16,256]{2,1,0:T(8,128)}), f32[16,16,256]{2,1,0:T(8,128)S(1)}, u32[]{:S(2)}, u32[]{:S(2)}) async-start(f32[16,16,256]{2,1,0:T(8,128)} %broadcast_in_dim.204), calls=%async_computation.3 | async-start | bytes 524288 | tf_op jit(solution)/shard_map/all_to_all | solution.py:39
  311.0 12.7 %all-to-all-start = ((f32[16,16,256]{2,1,0:T(8,128)}), f32[16,16,256]{2,1,0:T(8,128)S(1)}, u32[]{:S(2)}, u32[]{:S(2)}) async-start(f32[16,16,256]{2,1,0:T(8,128)} %broadcast_in_dim.201), calls=%async_computation | async-start | bytes 524288 | tf_op jit(solution)/shard_map/all_to_all | solution.py:39
  324.3 12.7 %all-to-all-start.1 = ((f32[16,16,256]{2,1,0:T(8,128)}), f32[16,16,256]{2,1,0:T(8,128)S(1)}, u32[]{:S(2)}, u32[]{:S(2)}) async-start(f32[16,16,256]{2,1,0:T(8,128)} %broadcast_in_dim.202), calls=%async_computation.1 | async-start | bytes 524288 | tf_op jit(solution)/shard_map/all_to_all | solution.py:39
  328.5 11.6 %copy-start.2 = (s32[256]{0:T(256)S(1)}, s32[256]{0:T(256)}, u32[]{:S(2)}) copy-start(s32[256]{0:T(256)} %iota_add_fusion) | copy-start | bytes 3076
  328.5 11.6 %copy-start.4 = (pred[256]{0:T(512)(128)(4,1)S(1)}, pred[256]{0:T(512)(128)(4,1)}, u32[]{:S(2)}) copy-start(pred[256]{0:T(512)(128)(4,1)} %dynamic_slice.108) | copy-start | bytes 772
  338.7 1.4 copy-start.1
  520.2 2.4 copy-start.3
  525.2 2.4 copy-start.3
  530.2 2.4 copy-start.3
  535.2 2.4 copy-start.3
Sparse Core Ops, SparseCore 0:
  10.7 104.3 all-gather.1
where the time goes:
time: 556 us; the launch traced here: 549 us
  matrix products  232 us (42%)
  waiting for transfers between devices  126 us (23%)
  local copies, waits for them, and re-layouts  84.4 us (15%)
  blocking collectives  33.9 us (6%)
  other arithmetic  29 us (5%)
  starting transfers between devices  20.8 us (4%)
  between operations  18.3 us (3%)
    all_gather x1, waiting for transfers between devices, in_one_piece(): filled = lax.all_gather(both, axis, axis=dim, tiled=True)  102 us
    dot_general x67, matrix products, tile_logits(): jnp.einsum('rhd,khd->hrk', query_set[1], key_set[1], preferred_element_ty...  92 us
    dot_general x30, matrix products, key_side(): jnp.einsum('hrk,rhd->khd', weights, query_set[1], preferred_element_type=...  86.6 us
    dot_general x33, matrix products, tile_logits(): jnp.einsum('rhd,khd->hrk', query_set[0], key_set[0], preferred_element_ty...  43.2 us
    psum x5, blocking collectives, one_axis_at_a_time(): shard = lax.psum(shard, axis)  33.9 us
    dynamic_slice x69, local copies, waits for them, and re-layouts, select(): lax.dynamic_slice_in_dim(is_real, row_start, row_count, 0)  28.6 us
    all_to_all x4, waiting for transfers between devices, sent_to_all(): lax.all_to_all(jnp.broadcast_to(shard[None], (size, *shard.shape)), axis,...  24.4 us
    dynamic_slice x60, local copies, waits for them, and re-layouts, key_side(): lax.dynamic_slice_in_dim(member, query_start, half_rows, 1)  22.1 us
  transfers between devices with their start and end apart: 5, of which 5 were waited for; matrix products, arithmetic and copies ran while one was open for 1% of the time, Pallas kernels for 0%

commit v1 on v0

v1 whole, which is shorter than its diff:
```python
import functools

import jax
import jax.numpy as jnp
from jax import lax
from jax.experimental import pallas as pl
from jax.experimental.pallas import tpu as pltpu
from jax.sharding import PartitionSpec as P

H_REL = 128
LIVE = 3072
TILE = 256
LANES = 128
LOG2E = 1.4426950408889634
LN2 = 0.6931471805599453
NEGATIVE = -1e30
MESH = pl.DeviceIdType.MESH
F32 = jnp.float32
BF16 = jnp.bfloat16


def greet(peers):
    barrier = pltpu.get_barrier_semaphore()
    for peer in peers:
        pl.semaphore_signal(barrier, inc=1, device_id=peer, device_id_type=MESH)
    pl.semaphore_wait(barrier, len(peers))


def others(axis, n):
    me = lax.axis_index(axis)
    return me, [lax.rem(me + k, n) for k in range(1, n)]


def send(src, dst, send_sem, recv_sem, device):
    copy = pltpu.make_async_remote_copy(
        src_ref=src, dst_ref=dst, send_sem=send_sem, recv_sem=recv_sem,
        device_id=device, device_id_type=MESH,
    )
    copy.start()
    return copy


def exchange_kernel(n, x_ref, r_ref, send_sem, recv_sem, own_sem):
    me, peers = others("seq", n)
    own = pltpu.make_async_copy(x_ref.at[me], r_ref.at[me], own_sem)
    own.start()
    greet([{"seq": p} for p in peers])
    copies = [
        send(x_ref.at[p], r_ref.at[me], send_sem.at[k], recv_sem.at[k], {"seq": p})
        for k, p in enumerate(peers)
    ]
    own.wait()
    for copy in copies:
        copy.wait()


def exchange(x, n):
    any_space = pl.BlockSpec(memory_space=pl.ANY)
    return pl.pallas_call(
        functools.partial(exchange_kernel, n),
        out_shape=jax.ShapeDtypeStruct(x.shape, x.dtype),
        in_specs=[any_space],
        out_specs=any_space,
        scratch_shapes=[
            pltpu.SemaphoreType.DMA((n - 1,)),
            pltpu.SemaphoreType.DMA((n - 1,)),
            pltpu.SemaphoreType.DMA,
        ],
        compiler_params=pltpu.CompilerParams(collective_id=0, has_side_effects=True),
    )(x)


def finish_kernel(n, m, x_ref, part_ref, r_ref, total_ref, row, grid, sems):
    send_sem, recv_sem, seq_send, seq_recv, head_send, head_recv, own_sem = sems
    me, peers = others("seq", n)
    my_head, head_peers = others("head", m)
    own = pltpu.make_async_copy(x_ref.at[me], r_ref.at[me], own_sem.at[0])
    own.start()
    mine = pltpu.make_async_copy(part_ref, row.at[me], own_sem.at[1])
    mine.start()
    greet([{"seq": p} for p in peers] + [{"head": p} for p in head_peers])
    parts = [
        send(part_ref, row.at[me], seq_send.at[k], seq_recv.at[k], {"seq": p})
        for k, p in enumerate(peers)
    ]
    copies = [
        send(x_ref.at[p], r_ref.at[me], send_sem.at[k], recv_sem.at[k], {"seq": p})
        for k, p in enumerate(peers)
    ]
    mine.wait()
    for copy in parts:
        copy.wait()
    keep = pltpu.make_async_copy(row, grid.at[my_head], own_sem.at[1])
    keep.start()
    rows = [
        send(row, grid.at[my_head], head_send.at[k], head_recv.at[k], {"head": p})
        for k, p in enumerate(head_peers)
    ]
    keep.wait()
    for copy in rows:
        copy.wait()
    total_ref[...] = jnp.sum(jnp.sum(grid[...], axis=(0, 1)), axis=1, keepdims=True)
    own.wait()
    for copy in copies:
        copy.wait()


def finish(x, part, n, m):
    any_space = pl.BlockSpec(memory_space=pl.ANY)
    dma = pltpu.SemaphoreType.DMA
    return pl.pallas_call(
        functools.partial(finish_kernel, n, m),
        out_shape=(
            jax.ShapeDtypeStruct(x.shape, x.dtype),
            jax.ShapeDtypeStruct((1, 1), F32),
        ),
        in_specs=[any_space, any_space],
        out_specs=(any_space, pl.BlockSpec(memory_space=pltpu.VMEM)),
        scratch_shapes=[
            pltpu.VMEM((n, 1, LANES), F32),
            pltpu.VMEM((m, n, 1, LANES), F32),
            [
                dma((n - 1,)), dma((n - 1,)), dma((n - 1,)), dma((n - 1,)),
                dma((m - 1,)), dma((m - 1,)), dma((2,)),
            ],
        ],
        compiler_params=pltpu.CompilerParams(collective_id=1, has_side_effects=True),
    )(x, part)


def head_kernel(dt, ds, counts, x_ref, g_ref, part_ref, packed, rows, t_ref, s_ref, grad):
    blocks = x_ref.shape[0]
    depth = dt + ds
    scale = ds ** -0.5
    t_scale, s_scale = dt ** -0.5 * LOG2E, scale * LOG2E
    lane = lax.broadcasted_iota(jnp.int32, (depth, LANES), 1)

    packed[...] = jnp.zeros_like(packed)
    start = jnp.int32(0)
    for b in range(blocks):
        shift = lax.rem(start, LANES)
        base = pl.multiple_of(start - shift, LANES)
        first = pltpu.roll(x_ref[b, :, :LANES].astype(F32), shift, 1)
        second = pltpu.roll(x_ref[b, :, LANES:].astype(F32), shift, 1)
        late = lane >= shift
        here = pl.ds(base, LANES)
        packed[:depth, here] = jnp.where(late, first, packed[:depth, here])
        packed[:depth, pl.ds(base + LANES, LANES)] = jnp.where(late, second, first)
        packed[:depth, pl.ds(base + 2 * LANES, LANES)] = second
        start = start + counts[b]
    for c in range(LIVE // TILE):
        here = slice(c * TILE, (c + 1) * TILE)
        rows[here, :] = packed[:, here].T.astype(BF16)
    grad[...] = jnp.zeros_like(grad)

    feature = lax.broadcasted_iota(jnp.int32, (LANES, TILE), 0)
    causal = lax.broadcasted_iota(jnp.int32, (TILE, TILE), 0) <= lax.broadcasted_iota(
        jnp.int32, (TILE, TILE), 1
    )

    def at(c):
        return pl.ds(pl.multiple_of(c * TILE, TILE), TILE)

    def row_block(i, loss):
        query = packed[:, at(i)]
        t_query = jnp.where(feature < dt, query, 0.0).astype(BF16)
        s_query = jnp.where(feature < dt, 0.0, query).astype(BF16)
        s_own = query[dt:depth].astype(BF16)

        def logits(j):
            key = rows[at(j), :]
            t = jnp.dot(key, t_query, preferred_element_type=F32) * t_scale
            s = jnp.dot(key, s_query, preferred_element_type=F32) * s_scale
            return t, s

        t, s = logits(i)
        t = jnp.where(causal, t, NEGATIVE)
        s = jnp.where(causal, s, NEGATIVE)
        t_ref[at(i), :] = t
        s_ref[at(i), :] = s

        def fold(v, op):
            return op(v.reshape(TILE // 8, 8, TILE), axis=0)

        def tops(j, tops_so_far):
            t, s = logits(j)
            t_ref[at(j), :] = t
            s_ref[at(j), :] = s
            return (
                jnp.maximum(tops_so_far[0], fold(t, jnp.max)),
                jnp.maximum(tops_so_far[1], fold(s, jnp.max)),
            )

        t_top, s_top = lax.fori_loop(0, i, tops, (fold(t, jnp.max), fold(s, jnp.max)))
        t_top = jnp.max(t_top, axis=0, keepdims=True)
        s_top = jnp.max(s_top, axis=0, keepdims=True)

        def sums(j, so_far):
            t, s = t_ref[at(j), :], s_ref[at(j), :]
            pt = jnp.exp2(t - t_top)
            ps = jnp.exp2(s - s_top)
            t_ref[at(j), :] = pt
            s_ref[at(j), :] = ps
            return (
                so_far[0] + fold(pt, jnp.sum),
                so_far[1] + fold(ps, jnp.sum),
                so_far[2] + fold(pt * (t - s), jnp.sum),
            )

        zero = jnp.zeros((8, TILE), F32)
        t_sum, s_sum, cross = (
            jnp.sum(v, axis=0, keepdims=True)
            for v in lax.fori_loop(0, i + 1, sums, (zero, zero, zero))
        )
        kl = cross / t_sum - (t_top + jnp.log2(t_sum)) + (s_top + jnp.log2(s_sum))
        t_inv, s_inv = 1.0 / t_sum, 1.0 / s_sum

        def grads(j, query_grad):
            w = (s_ref[at(j), :] * s_inv - t_ref[at(j), :] * t_inv).astype(BF16)
            s_key = packed[dt:depth, at(j)].astype(BF16)
            grad[:, at(j)] += lax.dot_general(
                s_own, w, (((1,), (1,)), ((), ())), preferred_element_type=F32
            )
            return query_grad + jnp.dot(s_key, w, preferred_element_type=F32)

        query_grad = lax.fori_loop(0, i + 1, grads, jnp.zeros((ds, TILE), F32))
        grad[:, at(i)] += query_grad
        return loss + kl * LN2

    loss = lax.fori_loop(0, LIVE // TILE, row_block, jnp.zeros((1, TILE), F32))
    part_ref[0] = loss[:, :LANES] + loss[:, LANES:]

    lane = lax.broadcasted_iota(jnp.int32, (ds, LANES), 1)
    start = jnp.int32(0)
    for b in range(blocks):
        shift = lax.rem(start, LANES)
        base = pl.multiple_of(start - shift, LANES)
        back = lax.rem(LANES - shift, LANES)
        pieces = [
            pltpu.roll(grad[:, pl.ds(base + k * LANES, LANES)], back, 1) for k in range(3)
        ]
        for k in range(2):
            v = jnp.where(lane < LANES - shift, pieces[k], pieces[k + 1])
            v = jnp.where(lane + k * LANES < counts[b], v * scale, 0.0)
            g_ref[b, :, k * LANES:(k + 1) * LANES] = v.astype(BF16)
        start = start + counts[b]


def one_head(counts, x, dt, ds):
    blocks, depth, width = x.shape
    padded = LIVE + 3 * LANES
    vmem = pl.BlockSpec(memory_space=pltpu.VMEM)
    return pl.pallas_call(
        functools.partial(head_kernel, dt, ds),
        out_shape=(
            jax.ShapeDtypeStruct((blocks, ds, width), BF16),
            jax.ShapeDtypeStruct((1, 1, LANES), F32),
        ),
        in_specs=[pl.BlockSpec(memory_space=pltpu.SMEM), vmem],
        out_specs=(vmem, vmem),
        scratch_shapes=[
            pltpu.VMEM((LANES, padded), F32),
            pltpu.VMEM((LIVE, LANES), BF16),
            pltpu.VMEM((LIVE, TILE), F32),
            pltpu.VMEM((LIVE, TILE), F32),
            pltpu.VMEM((ds, padded), F32),
        ],
        compiler_params=pltpu.CompilerParams(vmem_limit_bytes=48 << 20),
    )(counts, x)


def local(teacher, student, counts):
    n, m = lax.axis_size("seq"), lax.axis_size("head")
    tokens = teacher.shape[0]
    dt, ds = teacher.shape[1] // n, student.shape[1] // n

    def by_head(x, d):
        return x.reshape(tokens, n, d).transpose(1, 2, 0)

    x = jnp.concatenate([by_head(teacher, dt), by_head(student, ds)], axis=1)
    x = exchange(x, n)
    grad, part = one_head(counts, x, dt, ds)
    grad, total = finish(grad, part[0], n, m)
    grad = grad.transpose(2, 0, 1).reshape(tokens, n * ds).astype(F32)
    loss = total[0, 0] / (H_REL * jnp.sum(counts).astype(F32))
    return grad, loss


def solution(mesh):
    return jax.shard_map(
        local,
        mesh=mesh,
        in_specs=(P("seq", "head"), P("seq", "head"), P()),
        out_specs=(P("seq", "head"), P()),
        check_vma=False,
    )
```

time: 556 us -> 85.9 us (0.15); the launches traced: 549 us -> 85.7 us
  matrix products: 232 us -> 0 us
  waiting for transfers between devices: 126 us -> 0 us
  local copies, waits for them, and re-layouts: 84.4 us -> 4.76 us
  Pallas kernels: 0 us -> 75.3 us
  blocking collectives: 33.9 us -> 0 us
  other arithmetic: 29 us -> 2.57 us
  starting transfers between devices: 20.8 us -> 0 us
  between operations: 18.3 us -> 3.06 us
    dot_general x134 -> x0, matrix products: 232 us -> none  [the longest x67 92 us: tile_logits(): jnp.einsum('rhd,khd->hrk', query_set[1], key_set[1], preferred_element_ty...]
    all_gather x1 -> x0, waiting for transfers between devices: 102 us -> none  [in_one_piece(): filled = lax.all_gather(both, axis, axis=dim, tiled=True)]
    pallas_call x0 -> x3, Pallas kernels: none -> 75.3 us  [the longest x1 41 us: one_head(): pl.pallas_call(functools.partial(head_kernel, dt, ds), out_shape=(jax.Sha...]
    dynamic_slice x202 -> x0, local copies, waits for them, and re-layouts: 61.4 us -> none  [the longest x69 28.6 us: select(): lax.dynamic_slice_in_dim(is_real, row_start, row_count, 0)]
    psum x5 -> x0, blocking collectives: 33.9 us -> none  [one_axis_at_a_time(): shard = lax.psum(shard, axis)]
    all_to_all x4 -> x0, waiting for transfers between devices: 24.4 us -> none  [sent_to_all(): lax.all_to_all(jnp.broadcast_to(shard[None], (size, *shard.shape)), axis,...]
    all_to_all x4 -> x0, starting transfers between devices: 20.8 us -> none  [sent_to_all(): lax.all_to_all(jnp.broadcast_to(shard[None], (size, *shard.shape)), axis,...]
    reduce_sum x36 -> x1, other arithmetic: 19.6 us -> 0.63 us  [local(): loss = total[0, 0] / (H_REL * jnp.sum(counts).astype(F32))]
  transfers between devices with their start and end apart: 5 -> 0, of which waited for: 5 -> 0; matrix products, arithmetic and copies ran while one was open for 1% -> 0% of each run, Pallas kernels for 0% -> 0%
where the time goes in v1:
time: 85.9 us; the launch traced here: 85.7 us
  Pallas kernels  75.3 us (88%)
  local copies, waits for them, and re-layouts  4.76 us (6%)
  between operations  3.06 us (4%)
  other arithmetic  2.57 us (3%)
    pallas_call x1, Pallas kernels, one_head(): pl.pallas_call(functools.partial(head_kernel, dt, ds), out_shape=(jax.Sha...  41 us
    pallas_call x1, Pallas kernels, exchange(): pl.pallas_call(functools.partial(exchange_kernel, n), out_shape=jax.Shape...  17.9 us
    pallas_call x1, Pallas kernels, finish(): pl.pallas_call(functools.partial(finish_kernel, n, m), out_shape=(jax.Sha...  16.4 us
    unnamed x13, local copies, waits for them, and re-layouts  4.76 us

profile of v1, /device:TPU:1, one launch (start us, length us, event | category | flops | bytes accessed | tf_op | source)
XLA Modules:
  0.0 85.7 jit_solution(12709697298281017262)
XLA Ops:
  0.6 0.0 copy-start.4
  0.6 1.3 %copy.5 = bf16[256,1024]{0,1:T(8,128)(2,1)S(1)} copy(bf16[256,1024]{1,0:T(8,128)(2,1)} %param.3) | data formatting | bytes 1048576 | tf_op args[0]
  1.9 0.0 copy-done.4
  1.9 0.1 copy.6
  2.1 0.9 %pad_maximum_fusion.x_ref = bf16[16,96,256]{2,1,0:T(8,128)(2,1)} fusion(bf16[16,32,256]{2,1,0:T(8,128)(2,1)S(1)} %bitcast.14, bf16[16,64,256]{2,1,0:T(8,128)(2,1)S(1)} %bitcast.12), kind=kLoop, calls=%fused_computation | loop fusion | flops 1572864 | bytes 1572864 | tf_op jit(solution)/shard_map/concatenate | solution.py:280
  3.0 0.0 copy-start.3
  3.0 17.9 %shard_map.50.x_ref = bf16[16,96,256]{2,1,0:T(8,128)(2,1)} custom-call(bf16[16,96,256]{2,1,0:T(8,128)(2,1)} %pad_maximum_fusion.x_ref), custom_call_target="tpu_custom_call" | custom-call | tf_op jit(solution)/shard_map/pallas_call | solution.py:59
  20.9 0.0 copy-done.3
  20.9 0.0 copy-start
  21.0 1.1 %copy-done = bf16[16,96,256]{2,1,0:T(8,128)(2,1)S(1)} copy-done((bf16[16,96,256]{2,1,0:T(8,128)(2,1)S(1)}, bf16[16,96,256]{2,1,0:T(8,128)(2,1)}, u32[]{:S(2)}) %copy-start) | copy-done | bytes 786456
  22.1 41.0 %shard_map.51 = (bf16[16,32,256]{2,1,0:T(8,128)(2,1)S(1)}, f32[1,1,128]{2,1,0:T(1,128)S(1)}) custom-call(s32[16]{0:T(128)S(1)} %copy-done.3, bf16[16,96,256]{2,1,0:T(8,128)(2,1)S(1)} %copy-done), custom_call_target="tpu_custom_call" | custom-call | tf_op jit(solution)/shard_map/pallas_call | solution.py:253
  63.1 0.0 copy-start.1
  63.1 0.7 copy-done.1
  63.8 0.0 copy-start.2
  63.8 0.5 copy-done.2
  64.3 16.4 %shard_map.52 = (bf16[16,32,256]{2,1,0:T(8,128)(2,1)}, f32[1,1]{1,0:T(1,128)}) custom-call(bf16[16,32,256]{2,1,0:T(8,128)(2,1)} %copy-done.1, f32[1,128]{1,0:T(1,128)} %bitcast.11), custom_call_target="tpu_custom_call" | custom-call | tf_op jit(solution)/shard_map/pallas_call | solution.py:111
  80.7 1.0 %convert_element_type.17 = f32[16,32,256]{2,1,0:T(8,128)S(1)} convert(bf16[16,32,256]{2,1,0:T(8,128)(2,1)} %get-tuple-element.8) | non-fusion elementwise | flops 131072 | bytes 786432 | tf_op jit(solution)/shard_map/convert_element_type | solution.py:284
  81.7 1.0 %copy.7 = f32[256,512]{1,0:T(8,128)} copy(f32[256,512]{0,1:T(8,128)S(1)} %bitcast.13) | data formatting | bytes 1048576
  82.7 0.6 reduce_sum.9
Async XLA Ops:
  0.6 1.3 %copy-start.4 = (bf16[256,512]{1,0:T(8,128)(2,1)S(1)}, bf16[256,512]{1,0:T(8,128)(2,1)}, u32[]{:S(2)}) copy-start(bf16[256,512]{1,0:T(8,128)(2,1)} %param.4) | copy-start | bytes 786436
  3.0 17.9 %copy-start.3 = (s32[16]{0:T(128)S(1)}, s32[16]{0:T(128)}, u32[]{:S(2)}) copy-start(s32[16]{0:T(128)} %counts.1) | copy-start | bytes 196
  20.9 1.1 %copy-start = (bf16[16,96,256]{2,1,0:T(8,128)(2,1)S(1)}, bf16[16,96,256]{2,1,0:T(8,128)(2,1)}, u32[]{:S(2)}) copy-start(bf16[16,96,256]{2,1,0:T(8,128)(2,1)} %shard_map.50.x_ref) | copy-start | bytes 2359300
  63.1 0.7 copy-start.1
  63.8 0.5 copy-start.2

commit v2 on v0

v2 whole, which is shorter than its diff:
```python
import functools

import jax
import jax.numpy as jnp
from jax import lax
from jax.experimental import pallas as pl
from jax.experimental.pallas import tpu as pltpu
from jax.sharding import PartitionSpec as P

H_REL = 128
LIVE = 3072
TILE = 256
LANES = 128
LOG2E = 1.4426950408889634
LN2 = 0.6931471805599453
NEGATIVE = -1e30
MESH = pl.DeviceIdType.MESH
F32 = jnp.float32
BF16 = jnp.bfloat16


def greet(peers):
    barrier = pltpu.get_barrier_semaphore()
    for peer in peers:
        pl.semaphore_signal(barrier, inc=1, device_id=peer, device_id_type=MESH)
    pl.semaphore_wait(barrier, len(peers))


def others(axis, n):
    me = lax.axis_index(axis)
    return me, [lax.rem(me + k, n) for k in range(1, n)]


def send(src, dst, send_sem, recv_sem, device):
    copy = pltpu.make_async_remote_copy(
        src_ref=src, dst_ref=dst, send_sem=send_sem, recv_sem=recv_sem,
        device_id=device, device_id_type=MESH,
    )
    copy.start()
    return copy


def own_start(counts, n):
    me = lax.axis_index("seq")
    start = jnp.int32(0)
    for b in range(n - 1):
        start = start + jnp.where(b < me, counts[b], 0)
    return me, lax.rem(start, TILE)


def enter_kernel(n, counts, t_ref, s_ref, o_ref):
    _, shift = own_start(counts, n)
    dt = t_ref.shape[1] // n
    for ref, row in ((t_ref, 0), (s_ref, dt)):
        d = ref.shape[1] // n
        for c in range(ref.shape[1] // LANES):
            part = ref[:, c * LANES:(c + 1) * LANES].astype(F32).T
            part = pltpu.roll(part, shift, 1).astype(BF16)
            for k in range(LANES // d):
                o_ref[c * (LANES // d) + k, row:row + d, :] = part[k * d:(k + 1) * d]


def leave_kernel(n, scale, counts, g_ref, total_ref, o_ref, loss_ref):
    me, shift = own_start(counts, n)
    back = lax.rem(TILE - shift, TILE)
    ds = g_ref.shape[1]
    per = LANES // ds
    lane = lax.broadcasted_iota(jnp.int32, (LANES, TILE), 1)
    real = jnp.int32(0)
    whole = jnp.int32(0)
    for b in range(n):
        real = real + jnp.where(b == me, counts[b], 0)
        whole = whole + counts[b]
    for c in range(n // per):
        part = g_ref[c * per:(c + 1) * per].astype(F32).reshape(LANES, TILE)
        part = jnp.where(lane < real, pltpu.roll(part, back, 1) * scale, 0.0)
        o_ref[:, c * LANES:(c + 1) * LANES] = part.T
    loss_ref[...] = total_ref[...] / (H_REL * whole.astype(F32))


def pack(starts, spare, x_ref, packed, rows, dt):
    blocks, depth, width = x_ref.shape
    lane = lax.broadcasted_iota(jnp.int32, (depth, TILE), 1)
    for c in range(LIVE // TILE):
        v = None
        for b in range(c, min(blocks, c + spare + 1)):
            piece = x_ref[b].astype(F32)
            v = piece if v is None else jnp.where(lane >= starts[b] - c * TILE, piece, v)
        here = slice(c * TILE, (c + 1) * TILE)
        packed[:, here] = v
        t, s = v[:dt], v[dt:]
        rows[here, :] = jnp.concatenate([t, t, t, s, s], axis=0).T.astype(BF16)


def pieces(x, count):
    out = []
    for k in range(count):
        out.append(x.astype(BF16))
        x = x - out[-1].astype(F32)
    return out


def at(c):
    return pl.ds(pl.multiple_of(c * TILE, TILE), TILE)


def tile_of(i, j):
    return lax.div(i * (i + 1), 2) + j


def fold(v, op):
    return op(v.reshape(TILE // 8, 8, TILE), axis=0)


def statistics(i, dt, packed, rows, pt_ref, ps_ref, tops, stats):
    ds = packed.shape[0] - dt
    query = packed[:, at(i)]
    t_query = pieces(query[:dt] * (dt ** -0.5 * LOG2E), 3)
    s_query = pieces(query[dt:] * (ds ** -0.5 * LOG2E), 2)
    t_zero, s_zero = jnp.zeros((3 * dt, TILE), BF16), jnp.zeros((2 * ds, TILE), BF16)
    t_query = jnp.concatenate(t_query + [s_zero], axis=0)
    s_query = jnp.concatenate([t_zero] + s_query, axis=0)
    causal = lax.broadcasted_iota(jnp.int32, (TILE, TILE), 0) <= lax.broadcasted_iota(
        jnp.int32, (TILE, TILE), 1
    )

    def one_tile(j, state, diagonal):
        key = rows[at(j), :]
        t = jnp.dot(key, t_query, preferred_element_type=F32)
        s = jnp.dot(key, s_query, preferred_element_type=F32)
        if diagonal:
            t = jnp.where(causal, t, NEGATIVE)
            s = jnp.where(causal, s, NEGATIVE)
        t = t.reshape(TILE // 8, 8, TILE)
        s = s.reshape(TILE // 8, 8, TILE)
        t_top, s_top = jnp.max(t, axis=0), jnp.max(s, axis=0)
        if not diagonal:
            t_top = jnp.maximum(t_top, state[0])
            s_top = jnp.maximum(s_top, state[1])
        pt = jnp.exp2(t - t_top)
        ps = jnp.exp2(s - s_top)
        here = tile_of(i, j)
        pt_ref[here] = pt
        ps_ref[here] = ps
        tops[here, 0] = t_top
        tops[here, 1] = s_top
        t_sum, s_sum = jnp.sum(pt, axis=0), jnp.sum(ps, axis=0)
        cross = jnp.sum(pt * (t - s), axis=0)
        if not diagonal:
            t_less = jnp.exp2(state[0] - t_top)
            t_sum = t_sum + state[2] * t_less
            cross = cross + state[3] * t_less
            s_sum = s_sum + state[4] * jnp.exp2(state[1] - s_top)
        return t_top, s_top, t_sum, cross, s_sum

    state = one_tile(i, None, True)
    t8, s8, t_sum, cross, s_sum = lax.fori_loop(
        0, i, lambda j, state: one_tile(j, state, False), state
    )
    t_top = jnp.max(t8, axis=0, keepdims=True)
    s_top = jnp.max(s8, axis=0, keepdims=True)
    t_less = jnp.exp2(t8 - t_top)
    t_sum = jnp.sum(t_sum * t_less, axis=0, keepdims=True)
    cross = jnp.sum(cross * t_less, axis=0, keepdims=True)
    s_sum = jnp.sum(s_sum * jnp.exp2(s8 - s_top), axis=0, keepdims=True)
    kl = cross / t_sum - (t_top + jnp.log2(t_sum)) + (s_top + jnp.log2(s_sum))
    stats[i] = jnp.concatenate([t_top, s_top, 1.0 / t_sum, 1.0 / s_sum], axis=0)
    return kl * LN2


def gradients(i, dt, packed, pt_ref, ps_ref, tops, stats, grad):
    s_own = packed[dt:, at(i)].astype(BF16)
    t_top, s_top, t_inv, s_inv = (stats[i, pl.ds(k, 1), :] for k in range(4))

    def one_tile(j, query_grad):
        here = tile_of(i, j)
        t_scale = jnp.exp2(tops[here, 0] - t_top) * t_inv
        s_scale = jnp.exp2(tops[here, 1] - s_top) * s_inv
        w = ps_ref[here] * s_scale - pt_ref[here] * t_scale
        w = w.reshape(TILE, TILE).astype(BF16)
        s_key = packed[dt:, at(j)].astype(BF16)
        grad[j] += lax.dot_general(
            s_own, w, (((1,), (1,)), ((), ())), preferred_element_type=F32
        )
        return query_grad + jnp.dot(s_key, w, preferred_element_type=F32)

    query_grad = lax.fori_loop(0, i + 1, one_tile, jnp.zeros(grad.shape[1:], F32))
    grad[i] += query_grad


def kernel(
    dt, n, m, counts, x_ref, g_ref, total_ref,
    x_in, packed, rows, pt_ref, ps_ref, tops, stats, grad, g_out, starts, part, row, grid, sems,
):
    x_send, x_recv, g_send, g_recv, seq_send, seq_recv, head_send, head_recv, own = sems
    blocks = LIVE // TILE
    spare = n - blocks
    me, peers = others("seq", n)
    my_head, head_peers = others("head", m)
    own_x = pltpu.make_async_copy(x_ref.at[me], x_in.at[me], own.at[0])
    own_x.start()
    greet([{"seq": p} for p in peers] + [{"head": p} for p in head_peers])
    copies = [
        send(x_ref.at[p], x_in.at[me], x_send.at[k], x_recv.at[k], {"seq": p})
        for k, p in enumerate(peers)
    ]
    start = jnp.int32(0)
    scalars = []
    for b in range(n):
        starts[b] = start
        scalars.append(start)
        start = start + counts[b]
    grad[...] = jnp.zeros_like(grad)
    own_x.wait()
    for copy in copies:
        copy.wait()

    pack(scalars, spare, x_in, packed, rows, dt)
    loss = lax.fori_loop(
        0, blocks,
        lambda i, loss: loss + statistics(i, dt, packed, rows, pt_ref, ps_ref, tops, stats),
        jnp.zeros((1, TILE), F32),
    )
    part[...] = loss[:, :LANES] + loss[:, LANES:]

    def finish_block(b):
        lane = lax.broadcasted_iota(jnp.int32, grad.shape[1:], 1)
        first = starts[b]
        top = blocks - 1
        v = grad[jnp.minimum(b, top)]
        for k in range(1, spare + 1):
            c = jnp.clip(b - k, 0, top)
            v = jnp.where(lane + c * TILE >= first, grad[c], v)
        g_out[b] = v.astype(BF16)

    def to_owner(b):
        @pl.when(b == me)
        def _():
            pltpu.make_async_copy(g_out.at[b], g_ref.at[me], own.at[1]).start()

        @pl.when(b != me)
        def _():
            send(g_out.at[b], g_ref.at[me], g_send.at[b], g_recv.at[me], {"seq": b})

    def down(k, _):
        i = blocks - 1 - k
        gradients(i, dt, packed, pt_ref, ps_ref, tops, stats, grad)

        @pl.when(k > 0)
        def _():
            to_owner(i + spare + 1)

        finish_block(i + spare)
        return 0

    lax.fori_loop(0, 1, down, 0)
    own_part = pltpu.make_async_copy(part, row.at[me], own.at[0])
    own_part.start()
    parts = [
        send(part, row.at[me], seq_send.at[k], seq_recv.at[k], {"seq": p})
        for k, p in enumerate(peers)
    ]
    lax.fori_loop(1, 6, down, 0)
    own_part.wait()
    for copy in parts:
        copy.wait()
    own_row = pltpu.make_async_copy(row, grid.at[my_head], own.at[0])
    own_row.start()
    row_copies = [
        send(row, grid.at[my_head], head_send.at[k], head_recv.at[k], {"head": p})
        for k, p in enumerate(head_peers)
    ]
    lax.fori_loop(6, blocks, down, 0)
    for b in range(spare):
        finish_block(b)
    for b in range(spare, -1, -1):
        to_owner(b)
    own_row.wait()
    for copy in row_copies:
        copy.wait()
    total_ref[...] = jnp.sum(jnp.sum(grid[...], axis=(0, 1)), axis=1, keepdims=True)
    pltpu.make_async_copy(g_out.at[me], g_ref.at[me], own.at[1]).wait()
    for p in peers:
        pltpu.make_async_remote_copy(
            src_ref=g_out.at[p], dst_ref=g_ref.at[p], send_sem=g_send.at[p],
            recv_sem=g_recv.at[p], device_id={"seq": p}, device_id_type=MESH,
        ).wait()


def local(teacher, student, counts):
    n, m = lax.axis_size("seq"), lax.axis_size("head")
    tokens = teacher.shape[0]
    dt, ds = teacher.shape[1] // n, student.shape[1] // n
    depth = dt + ds
    blocks = LIVE // TILE
    tiles = blocks * (blocks + 1) // 2
    vmem = pl.BlockSpec(memory_space=pltpu.VMEM)
    smem = pl.BlockSpec(memory_space=pltpu.SMEM)
    any_space = pl.BlockSpec(memory_space=pl.ANY)
    dma = pltpu.SemaphoreType.DMA
    x = pl.pallas_call(
        functools.partial(enter_kernel, n),
        out_shape=jax.ShapeDtypeStruct((n, depth, tokens), BF16),
        in_specs=[smem, vmem, vmem],
        out_specs=vmem,
    )(counts, teacher, student)
    grad, total = pl.pallas_call(
        functools.partial(kernel, dt, n, m),
        out_shape=(
            jax.ShapeDtypeStruct((n, ds, tokens), BF16),
            jax.ShapeDtypeStruct((1, 1), F32),
        ),
        in_specs=[smem, any_space],
        out_specs=(any_space, vmem),
        scratch_shapes=[
            pltpu.VMEM((n, depth, tokens), BF16),
            pltpu.VMEM((depth, LIVE), F32),
            pltpu.VMEM((LIVE, 3 * dt + 2 * ds), BF16),
            pltpu.VMEM((tiles, TILE // 8, 8, TILE), F32),
            pltpu.VMEM((tiles, TILE // 8, 8, TILE), F32),
            pltpu.VMEM((tiles, 2, 8, TILE), F32),
            pltpu.VMEM((blocks, 4, TILE), F32),
            pltpu.VMEM((blocks, ds, TILE), F32),
            pltpu.VMEM((n, ds, tokens), BF16),
            pltpu.SMEM((n,), jnp.int32),
            pltpu.VMEM((1, LANES), F32),
            pltpu.VMEM((n, 1, LANES), F32),
            pltpu.VMEM((m, n, 1, LANES), F32),
            [dma((n - 1,))] * 2 + [dma((n,))] * 2 + [dma((n - 1,))] * 2
            + [dma((m - 1,))] * 2 + [dma((2,))],
        ],
        compiler_params=pltpu.CompilerParams(
            collective_id=0, has_side_effects=True, vmem_limit_bytes=60 << 20
        ),
    )(counts, x)
    grad, loss = pl.pallas_call(
        functools.partial(leave_kernel, n, ds ** -0.5),
        out_shape=(
            jax.ShapeDtypeStruct((tokens, n * ds), F32),
            jax.ShapeDtypeStruct((1, 1), F32),
        ),
        in_specs=[smem, vmem, vmem],
        out_specs=(vmem, vmem),
    )(counts, grad, total)
    return grad, loss.reshape(())


def solution(mesh):
    return jax.shard_map(
        local,
        mesh=mesh,
        in_specs=(P("seq", "head"), P("seq", "head"), P()),
        out_specs=(P("seq", "head"), P()),
        check_vma=False,
    )
```

time: 556 us -> 77.9 us (0.14); the launches traced: 549 us -> 77.7 us
  matrix products: 232 us -> 0 us
  waiting for transfers between devices: 126 us -> 0 us
  local copies, waits for them, and re-layouts: 84.4 us -> 0 us
  Pallas kernels: 0 us -> 77.1 us
  blocking collectives: 33.9 us -> 0 us
  other arithmetic: 29 us -> 0 us
  starting transfers between devices: 20.8 us -> 0 us
  between operations: 18.3 us -> 0.64 us
    dot_general x134 -> x0, matrix products: 232 us -> none  [the longest x67 92 us: tile_logits(): jnp.einsum('rhd,khd->hrk', query_set[1], key_set[1], preferred_element_ty...]
    all_gather x1 -> x0, waiting for transfers between devices: 102 us -> none  [in_one_piece(): filled = lax.all_gather(both, axis, axis=dim, tiled=True)]
    pallas_call x0 -> x3, Pallas kernels: none -> 77.1 us  [the longest x1 71.7 us: local(): pl.pallas_call(functools.partial(kernel, dt, n, m), out_shape=(jax.ShapeD...]
    dynamic_slice x202 -> x0, local copies, waits for them, and re-layouts: 61.4 us -> none  [the longest x69 28.6 us: select(): lax.dynamic_slice_in_dim(is_real, row_start, row_count, 0)]
    psum x5 -> x0, blocking collectives: 33.9 us -> none  [one_axis_at_a_time(): shard = lax.psum(shard, axis)]
    all_to_all x4 -> x0, waiting for transfers between devices: 24.4 us -> none  [sent_to_all(): lax.all_to_all(jnp.broadcast_to(shard[None], (size, *shard.shape)), axis,...]
    all_to_all x4 -> x0, starting transfers between devices: 20.8 us -> none  [sent_to_all(): lax.all_to_all(jnp.broadcast_to(shard[None], (size, *shard.shape)), axis,...]
    reduce_sum x36 -> x0, other arithmetic: 19.6 us -> none  [the longest x33 18.1 us: advance(): jnp.sum(teacher_weight * (teacher_logits - student_logits), axis=2)]
  transfers between devices with their start and end apart: 5 -> 0, of which waited for: 5 -> 0; matrix products, arithmetic and copies ran while one was open for 1% -> 0% of each run, Pallas kernels for 0% -> 0%
where the time goes in v2:
time: 77.9 us; the launch traced here: 77.7 us
  Pallas kernels  77.1 us (99%)
    pallas_call x1, Pallas kernels, local(): pl.pallas_call(functools.partial(kernel, dt, n, m), out_shape=(jax.ShapeD...  71.7 us
    pallas_call x1, Pallas kernels, local(): pl.pallas_call(functools.partial(leave_kernel, n, ds ** (-0.5)), out_shap...  2.71 us
    pallas_call x1, Pallas kernels, local(): pl.pallas_call(functools.partial(enter_kernel, n), out_shape=jax.ShapeDty...  2.64 us

profile of v2, /device:TPU:1, one launch (start us, length us, event | category | flops | bytes accessed | tf_op | source)
XLA Modules:
  0.0 77.7 jit_solution(9728826277917168525)
XLA Ops:
  0.6 2.6 %shard_map.50.x_ref = bf16[16,96,256]{2,1,0:T(8,128)(2,1)} custom-call(s32[16]{0:T(128)} %counts.5, bf16[256,1024]{1,0:T(8,128)(2,1)} %t_ref.1, bf16[256,512]{1,0:T(8,128)(2,1)} %s_ref.1), custom_call_target="tpu_custom_call" | custom-call | tf_op jit(solution)/shard_map/pallas_call | solution.py:301
  3.3 71.7 %shard_map.51 = (bf16[16,32,256]{2,1,0:T(8,128)(2,1)}, f32[1,1]{1,0:T(1,128)}) custom-call(s32[16]{0:T(128)} %counts.5, bf16[16,96,256]{2,1,0:T(8,128)(2,1)} %shard_map.50.x_ref), custom_call_target="tpu_custom_call" | custom-call | tf_op jit(solution)/shard_map/pallas_call | solution.py:307
  75.0 2.7 %shard_map.52 = (f32[256,512]{1,0:T(8,128)}, f32[1,1]{1,0:T(1,128)}) custom-call(s32[16]{0:T(128)} %counts.5, bf16[16,32,256]{2,1,0:T(8,128)(2,1)} %get-tuple-element.6.g_ref, f32[1,1]{1,0:T(1,128)} %get-tuple-element.7.total_ref), custom_call_target="tpu_custom_call" | custom-call | tf_op jit(solution)/shard_map/pallas_call | solution.py:336

commit v3 on v2

--- a/solution.py
+++ b/solution.py
@@ -78,18 +78,22 @@
     loss_ref[...] = total_ref[...] / (H_REL * whole.astype(F32))
 
 
-def pack(starts, spare, x_ref, packed, rows, dt):
+def pack(starts, spare, x_ref, students, rows, weights, dt):
     blocks, depth, width = x_ref.shape
+    ds = depth - dt
     lane = lax.broadcasted_iota(jnp.int32, (depth, TILE), 1)
     for c in range(LIVE // TILE):
         v = None
         for b in range(c, min(blocks, c + spare + 1)):
             piece = x_ref[b].astype(F32)
             v = piece if v is None else jnp.where(lane >= starts[b] - c * TILE, piece, v)
-        here = slice(c * TILE, (c + 1) * TILE)
-        packed[:, here] = v
         t, s = v[:dt], v[dt:]
-        rows[here, :] = jnp.concatenate([t, t, t, s, s], axis=0).T.astype(BF16)
+        rows[c] = jnp.concatenate([t, t, s, s, s, s], axis=0).T.astype(BF16)
+        students[c] = s.astype(BF16)
+        weights[c, 0] = jnp.concatenate(pieces(t * (dt ** -0.5 * LOG2E), 2), axis=0)
+        weights[c, 1] = jnp.concatenate(
+            pieces(s * (ds ** -0.5 * LOG2E), 3) + [jnp.zeros((ds, TILE), BF16)], axis=0
+        )
 
 
 def pieces(x, count):
@@ -108,89 +112,181 @@
     return lax.div(i * (i + 1), 2) + j
 
 
-def fold(v, op):
-    return op(v.reshape(TILE // 8, 8, TILE), axis=0)
-
-
-def statistics(i, dt, packed, rows, pt_ref, ps_ref, tops, stats):
-    ds = packed.shape[0] - dt
-    query = packed[:, at(i)]
-    t_query = pieces(query[:dt] * (dt ** -0.5 * LOG2E), 3)
-    s_query = pieces(query[dt:] * (ds ** -0.5 * LOG2E), 2)
-    t_zero, s_zero = jnp.zeros((3 * dt, TILE), BF16), jnp.zeros((2 * ds, TILE), BF16)
-    t_query = jnp.concatenate(t_query + [s_zero], axis=0)
-    s_query = jnp.concatenate([t_zero] + s_query, axis=0)
-    causal = lax.broadcasted_iota(jnp.int32, (TILE, TILE), 0) <= lax.broadcasted_iota(
-        jnp.int32, (TILE, TILE), 1
-    )
-
-    def one_tile(j, state, diagonal):
-        key = rows[at(j), :]
-        t = jnp.dot(key, t_query, preferred_element_type=F32)
-        s = jnp.dot(key, s_query, preferred_element_type=F32)
-        if diagonal:
-            t = jnp.where(causal, t, NEGATIVE)
-            s = jnp.where(causal, s, NEGATIVE)
-        t = t.reshape(TILE // 8, 8, TILE)
-        s = s.reshape(TILE // 8, 8, TILE)
-        t_top, s_top = jnp.max(t, axis=0), jnp.max(s, axis=0)
-        if not diagonal:
-            t_top = jnp.maximum(t_top, state[0])
-            s_top = jnp.maximum(s_top, state[1])
-        pt = jnp.exp2(t - t_top)
-        ps = jnp.exp2(s - s_top)
+def step(later, now, diagonal, rows, weights, into, source, tops, running, state, pt_ref, ps_ref):
+    now_at = [tile_of(*c) for c in now]
+    now_top = [(tops[here, 0], tops[here, 1]) for here in now_at]
+    sums = [[jnp.zeros(tops.shape[2:], F32)] * 3 for _ in now]
+    made = []
+    for i, j in later:
+        key = rows[j]
+        made.append([
+            jnp.dot(
+                key[:, k * LANES:(k + 1) * LANES], weights[i, k], preferred_element_type=F32
+            )
+            for k in range(2)
+        ])
+    tallest = [[None, None] for _ in later]
+    for g in range(TILE // 8):
+        for u, here in enumerate(now_at):
+            t, s = source[u, 0, g], source[u, 1, g]
+            pt = jnp.exp2(t - now_top[u][0])
+            ps = jnp.exp2(s - now_top[u][1])
+            pt_ref[here, g] = pt
+            ps_ref[here, g] = ps
+            sums[u] = [sums[u][0] + pt, sums[u][1] + ps, sums[u][2] + pt * (t - s)]
+        for u in range(len(later)):
+            for k in range(2):
+                v = made[u][k][g * 8:(g + 1) * 8]
+                if diagonal:
+                    row = lax.broadcasted_iota(jnp.int32, v.shape, 0) + g * 8
+                    v = jnp.where(row <= lax.broadcasted_iota(jnp.int32, v.shape, 1), v, NEGATIVE)
+                into[u, k, g] = v
+                tallest[u][k] = v if g == 0 else jnp.maximum(tallest[u][k], v)
+    for u, (i, j) in enumerate(later):
+        for k in range(2):
+            top = jnp.maximum(tallest[u][k], running[i, k])
+            running[i, k] = top
+            tops[tile_of(i, j), k] = top
+    for u, (i, _) in enumerate(now):
+        t_top, s_top = now_top[u]
+        t_less = jnp.exp2(state[i, 0] - t_top)
+        s_less = jnp.exp2(state[i, 1] - s_top)
+        state[i, 0] = t_top
+        state[i, 1] = s_top
+        state[i, 2] = state[i, 2] * t_less + sums[u][0]
+        state[i, 3] = state[i, 3] * s_less + sums[u][1]
+        state[i, 4] = state[i, 4] * t_less + sums[u][2]
+
+
+def by_parity(count, even, odd, run):
+    @pl.when(lax.rem(count, 2) == 0)
+    def _():
+        run(even, odd)
+
+    @pl.when(lax.rem(count, 2) == 1)
+    def _():
+        run(odd, even)
+
+
+def statistics(rows, weights, even, odd, pt_ref, ps_ref, tops, running, state, stats):
+    blocks = rows.shape[0]
+    running[...] = jnp.full(running.shape, NEGATIVE, F32)
+    state[:, :2] = jnp.full(running.shape, NEGATIVE, F32)
+    state[:, 2:] = jnp.zeros((blocks, 3, *running.shape[2:]), F32)
+
+    def sweep(first, after, tiles, diagonal):
+        def one(later, now, into, source):
+            step(
+                later, now, diagonal, rows, weights, into, source, tops, running, state,
+                pt_ref, ps_ref,
+            )
+
+        def trip(count, now):
+            later = [after(*now[-1])]
+            later.append(after(*later[0]))
+            by_parity(count, even, odd, lambda source, into: one(later, now, into, source))
+            return later
+
+        first = (jnp.int32(first[0]), jnp.int32(first[1]))
+        first = [first, after(*first)]
+        one(first, [], even, None)
+        trips = tiles // 2 - 1
+        now = lax.fori_loop(0, trips, trip, first)
+        one([], now, None, odd if trips % 2 else even)
+
+    def below(i, j):
+        wrap = j + 1 == i
+        return jnp.where(wrap, i + 1, i), jnp.where(wrap, 0, j + 1)
+
+    sweep((0, 0), lambda i, j: (i + 1, j + 1), blocks, True)
+    sweep((1, 0), below, blocks * (blocks - 1) // 2, False)
+
+    t8, s8, t_sum, s_sum, cross = (state[:, k] for k in range(5))
+    t_top = jnp.max(t8, axis=1, keepdims=True)
+    s_top = jnp.max(s8, axis=1, keepdims=True)
+    t_less = jnp.exp2(t8 - t_top)
+    t_sum = jnp.sum(t_sum * t_less, axis=1, keepdims=True)
+    cross = jnp.sum(cross * t_less, axis=1, keepdims=True)
+    s_sum = jnp.sum(s_sum * jnp.exp2(s8 - s_top), axis=1, keepdims=True)
+    kl = cross / t_sum - (t_top + jnp.log2(t_sum)) + (s_top + jnp.log2(s_sum))
+    stats[...] = jnp.concatenate([t_top, s_top, 1.0 / t_sum, 1.0 / s_sum], axis=1)
+    return jnp.sum(kl, axis=0) * LN2
+
+
+def back(i, j):
+    wrap = j == i
+    return jnp.where(wrap, i - 1, i), jnp.where(wrap, 0, j + 1)
+
+
+def gradient_step(later, now, into, source, students, pt_ref, ps_ref, tops, stats, grad):
+    nt = (((1,), (1,)), ((), ()))
+    parts = [
+        (
+            lax.dot_general(students[i], source[u], nt, preferred_element_type=F32),
+            jnp.dot(students[j], source[u], preferred_element_type=F32),
+        )
+        for u, (i, j) in enumerate(now)
+    ]
+    for u, (i, j) in enumerate(later):
         here = tile_of(i, j)
-        pt_ref[here] = pt
-        ps_ref[here] = ps
-        tops[here, 0] = t_top
-        tops[here, 1] = s_top
-        t_sum, s_sum = jnp.sum(pt, axis=0), jnp.sum(ps, axis=0)
-        cross = jnp.sum(pt * (t - s), axis=0)
-        if not diagonal:
-            t_less = jnp.exp2(state[0] - t_top)
-            t_sum = t_sum + state[2] * t_less
-            cross = cross + state[3] * t_less
-            s_sum = s_sum + state[4] * jnp.exp2(state[1] - s_top)
-        return t_top, s_top, t_sum, cross, s_sum
-
-    state = one_tile(i, None, True)
-    t8, s8, t_sum, cross, s_sum = lax.fori_loop(
-        0, i, lambda j, state: one_tile(j, state, False), state
-    )
-    t_top = jnp.max(t8, axis=0, keepdims=True)
-    s_top = jnp.max(s8, axis=0, keepdims=True)
-    t_less = jnp.exp2(t8 - t_top)
-    t_sum = jnp.sum(t_sum * t_less, axis=0, keepdims=True)
-    cross = jnp.sum(cross * t_less, axis=0, keepdims=True)
-    s_sum = jnp.sum(s_sum * jnp.exp2(s8 - s_top), axis=0, keepdims=True)
-    kl = cross / t_sum - (t_top + jnp.log2(t_sum)) + (s_top + jnp.log2(s_sum))
-    stats[i] = jnp.concatenate([t_top, s_top, 1.0 / t_sum, 1.0 / s_sum], axis=0)
-    return kl * LN2
-
-
-def gradients(i, dt, packed, pt_ref, ps_ref, tops, stats, grad):
-    s_own = packed[dt:, at(i)].astype(BF16)
-    t_top, s_top, t_inv, s_inv = (stats[i, pl.ds(k, 1), :] for k in range(4))
-
-    def one_tile(j, query_grad):
-        here = tile_of(i, j)
+        t_top, s_top, t_inv, s_inv = (stats[i, pl.ds(k, 1), :] for k in range(4))
         t_scale = jnp.exp2(tops[here, 0] - t_top) * t_inv
         s_scale = jnp.exp2(tops[here, 1] - s_top) * s_inv
-        w = ps_ref[here] * s_scale - pt_ref[here] * t_scale
-        w = w.reshape(TILE, TILE).astype(BF16)
-        s_key = packed[dt:, at(j)].astype(BF16)
-        grad[j] += lax.dot_general(
-            s_own, w, (((1,), (1,)), ((), ())), preferred_element_type=F32
-        )
-        return query_grad + jnp.dot(s_key, w, preferred_element_type=F32)
-
-    query_grad = lax.fori_loop(0, i + 1, one_tile, jnp.zeros(grad.shape[1:], F32))
-    grad[i] += query_grad
+        for g in range(0, TILE // 8, 2):
+            w = ps_ref[here, g:g + 2] * s_scale - pt_ref[here, g:g + 2] * t_scale
+            into[u, g * 8:g * 8 + 16, :] = w.reshape(16, TILE).astype(BF16)
+    for (i, j), (key_grad, query_grad) in zip(now, parts):
+        grad[j] += key_grad
+        grad[i] += query_grad
+
+
+def gradients(first, last, final, now, even, odd, students, pt_ref, ps_ref, tops, stats, grad, row_done):
+    def one(later, now, into, source):
+        gradient_step(later, now, into, source, students, pt_ref, ps_ref, tops, stats, grad)
+
+    def check(now):
+        for i, j in now:
+            pl.when(i == j)(functools.partial(row_done, i))
+
+    def trip(count, now):
+        later = [back(*now[-1])]
+        later.append(back(*later[0]))
+        by_parity(count, even, odd, lambda source, into: one(later, now, into, source))
+        check(now)
+        return later
+
+    now = lax.fori_loop(first, last - final, trip, now)
+    if final:
+        one([], now, None, odd if (last - 1) % 2 else even)
+        check(now)
+    return now
+
+
+def compute_scratch(dt, ds):
+    blocks = LIVE // TILE
+    tiles = blocks * (blocks + 1) // 2
+    return [
+        pltpu.VMEM((blocks, ds, TILE), BF16),
+        pltpu.VMEM((blocks, TILE, 2 * LANES), BF16),
+        pltpu.VMEM((blocks, 2, LANES, TILE), BF16),
+        pltpu.VMEM((2, 2, TILE // 8, 8, TILE), F32),
+        pltpu.VMEM((2, 2, TILE // 8, 8, TILE), F32),
+        pltpu.VMEM((tiles, TILE // 8, 8, TILE), F32),
+        pltpu.VMEM((tiles, TILE // 8, 8, TILE), F32),
+        pltpu.VMEM((tiles, 2, 8, TILE), F32),
+        pltpu.VMEM((blocks, 2, 8, TILE), F32),
+        pltpu.VMEM((blocks, 5, 8, TILE), F32),
+        pltpu.VMEM((blocks, 4, TILE), F32),
+        pltpu.VMEM((2, TILE, TILE), BF16),
+        pltpu.VMEM((2, TILE, TILE), BF16),
+        pltpu.VMEM((blocks, ds, TILE), F32),
+    ]
 
 
 def kernel(
     dt, n, m, counts, x_ref, g_ref, total_ref,
-    x_in, packed, rows, pt_ref, ps_ref, tops, stats, grad, g_out, starts, part, row, grid, sems,
+    x_in, students, rows, weights, even, odd, pt_ref, ps_ref, tops, running, state, stats,
+    w_even, w_odd, grad, g_out, starts, part, row, grid, sems,
 ):
     x_send, x_recv, g_send, g_recv, seq_send, seq_recv, head_send, head_recv, own = sems
     blocks = LIVE // TILE
@@ -215,12 +311,8 @@
     for copy in copies:
         copy.wait()
 
-    pack(scalars, spare, x_in, packed, rows, dt)
-    loss = lax.fori_loop(
-        0, blocks,
-        lambda i, loss: loss + statistics(i, dt, packed, rows, pt_ref, ps_ref, tops, stats),
-        jnp.zeros((1, TILE), F32),
-    )
+    pack(scalars, spare, x_in, students, rows, weights, dt)
+    loss = statistics(rows, weights, even, odd, pt_ref, ps_ref, tops, running, state, stats)
     part[...] = loss[:, :LANES] + loss[:, LANES:]
 
     def finish_block(b):
@@ -242,25 +334,29 @@
         def _():
             send(g_out.at[b], g_ref.at[me], g_send.at[b], g_recv.at[me], {"seq": b})
 
-    def down(k, _):
-        i = blocks - 1 - k
-        gradients(i, dt, packed, pt_ref, ps_ref, tops, stats, grad)
-
-        @pl.when(k > 0)
+    def row_done(i):
+        @pl.when(i + spare + 1 < n)
         def _():
             to_owner(i + spare + 1)
 
         finish_block(i + spare)
-        return 0
-
-    lax.fori_loop(0, 1, down, 0)
+
+    def run(first, last, final, now):
+        return gradients(
+            first, last, final, now, w_even, w_odd, students, pt_ref, ps_ref, tops, stats, grad, row_done
+        )
+
+    pairs = blocks * (blocks + 1) // 4
+    now = (jnp.int32(blocks - 1), jnp.int32(0))
+    now = [now, back(*now)]
+    gradient_step(now, [], w_even, None, students, pt_ref, ps_ref, tops, stats, grad)
     own_part = pltpu.make_async_copy(part, row.at[me], own.at[0])
     own_part.start()
     parts = [
         send(part, row.at[me], seq_send.at[k], seq_recv.at[k], {"seq": p})
         for k, p in enumerate(peers)
     ]
-    lax.fori_loop(1, 6, down, 0)
+    now = run(0, pairs // 2, False, now)
     own_part.wait()
     for copy in parts:
         copy.wait()
@@ -270,7 +366,7 @@
         send(row, grid.at[my_head], head_send.at[k], head_recv.at[k], {"head": p})
         for k, p in enumerate(head_peers)
     ]
-    lax.fori_loop(6, blocks, down, 0)
+    run(pairs // 2, pairs, True, now)
     for b in range(spare):
         finish_block(b)
     for b in range(spare, -1, -1):
@@ -292,8 +388,6 @@
     tokens = teacher.shape[0]
     dt, ds = teacher.shape[1] // n, student.shape[1] // n
     depth = dt + ds
-    blocks = LIVE // TILE
-    tiles = blocks * (blocks + 1) // 2
     vmem = pl.BlockSpec(memory_space=pltpu.VMEM)
     smem = pl.BlockSpec(memory_space=pltpu.SMEM)
     any_space = pl.BlockSpec(memory_space=pl.ANY)
@@ -314,13 +408,7 @@
         out_specs=(any_space, vmem),
         scratch_shapes=[
             pltpu.VMEM((n, depth, tokens), BF16),
-            pltpu.VMEM((depth, LIVE), F32),
-            pltpu.VMEM((LIVE, 3 * dt + 2 * ds), BF16),
-            pltpu.VMEM((tiles, TILE // 8, 8, TILE), F32),
-            pltpu.VMEM((tiles, TILE // 8, 8, TILE), F32),
-            pltpu.VMEM((tiles, 2, 8, TILE), F32),
-            pltpu.VMEM((blocks, 4, TILE), F32),
-            pltpu.VMEM((blocks, ds, TILE), F32),
+            *compute_scratch(dt, ds),
             pltpu.VMEM((n, ds, tokens), BF16),
             pltpu.SMEM((n,), jnp.int32),
             pltpu.VMEM((1, LANES), F32),

time: 77.9 us -> 60.8 us (0.78)
  Pallas kernels: 77.1 us -> 60 us
    pallas_call x1, Pallas kernels: 71.7 us -> 54.7 us  [local(): pl.pallas_call(functools.partial(kernel, dt, n, m), out_shape=(jax.ShapeD...]
where the time goes in v3:
time: 60.8 us; the launch traced here: 60.6 us
  Pallas kernels  60 us (99%)
  between operations  0.64 us (1%)
    pallas_call x1, Pallas kernels, local(): pl.pallas_call(functools.partial(kernel, dt, n, m), out_shape=(jax.ShapeD...  54.7 us
    pallas_call x1, Pallas kernels, local(): pl.pallas_call(functools.partial(leave_kernel, n, ds ** (-0.5)), out_shap...  2.71 us
    pallas_call x1, Pallas kernels, local(): pl.pallas_call(functools.partial(enter_kernel, n), out_shape=jax.ShapeDty...  2.64 us

profile of v3, /device:TPU:1, one launch (start us, length us, event | category | flops | bytes accessed | tf_op | source)
XLA Modules:
  0.0 60.6 jit_solution(9526672018464898123)
XLA Ops:
  0.6 2.6 %shard_map.50.x_ref = bf16[16,96,256]{2,1,0:T(8,128)(2,1)} custom-call(s32[16]{0:T(128)} %counts.5, bf16[256,1024]{1,0:T(8,128)(2,1)} %t_ref.1, bf16[256,512]{1,0:T(8,128)(2,1)} %s_ref.1), custom_call_target="tpu_custom_call" | custom-call | tf_op jit(solution)/shard_map/pallas_call | solution.py:395
  3.3 54.7 %shard_map.51 = (bf16[16,32,256]{2,1,0:T(8,128)(2,1)}, f32[1,1]{1,0:T(1,128)}) custom-call(s32[16]{0:T(128)} %counts.5, bf16[16,96,256]{2,1,0:T(8,128)(2,1)} %shard_map.50.x_ref), custom_call_target="tpu_custom_call" | custom-call | tf_op jit(solution)/shard_map/pallas_call | solution.py:401
  57.9 2.7 %shard_map.52 = (f32[256,512]{1,0:T(8,128)}, f32[1,1]{1,0:T(1,128)}) custom-call(s32[16]{0:T(128)} %counts.5, bf16[16,32,256]{2,1,0:T(8,128)(2,1)} %get-tuple-element.6.g_ref, f32[1,1]{1,0:T(1,128)} %get-tuple-element.7.total_ref), custom_call_target="tpu_custom_call" | custom-call | tf_op jit(solution)/shard_map/pallas_call | solution.py:424

commit v4 on v3

v4 whole, which is shorter than its diff:
```python
import functools

import jax
import jax.numpy as jnp
from jax import lax
from jax.experimental import pallas as pl
from jax.experimental.pallas import tpu as pltpu
from jax.sharding import PartitionSpec as P

H_REL = 128
LIVE = 3072
STUDENT_TILES = 6
TEACHER_TILES = 6
GRADIENT_TILES = 6
TILE = 256
LANES = 128
LOG2E = 1.4426950408889634
LN2 = 0.6931471805599453
NEGATIVE = -1e30
MESH = pl.DeviceIdType.MESH
F32 = jnp.float32
BF16 = jnp.bfloat16


def others(axis, n):
    me = lax.axis_index(axis)
    return me, [lax.rem(me + k, n) for k in range(1, n)]


def send(src, dst, send_sem, recv_sem, device):
    copy = pltpu.make_async_remote_copy(
        src_ref=src, dst_ref=dst, send_sem=send_sem, recv_sem=recv_sem,
        device_id=device, device_id_type=MESH,
    )
    copy.start()
    return copy


def pieces(x, count):
    out = []
    for k in range(count):
        out.append(x.astype(BF16))
        x = x - out[-1].astype(F32)
    return out


def tile_of(i, j):
    return lax.shift_right_logical(i * (i + 1), 1) + j


def own_start(counts, n):
    me = lax.axis_index("seq")
    start, real = jnp.int32(0), jnp.int32(0)
    for b in range(n):
        start = start + jnp.where(b < me, counts[b], 0)
        real = real + jnp.where(b == me, counts[b], 0)
    return start & (TILE - 1), real


def turn(shift, count):
    row = lax.broadcasted_iota(jnp.int32, (TILE, TILE), 0)
    lane = lax.broadcasted_iota(jnp.int32, (TILE, TILE), 1)
    hit = (lane == ((row + shift) & (TILE - 1))) & (row < count)
    return jnp.where(hit, 1.0, 0.0).astype(BF16)


def enter(x_ref, turned, x_out):
    d = x_out.shape[1]
    for c in range(x_ref.shape[1] // LANES):
        part = lax.dot_general(
            x_ref[:, c * LANES:(c + 1) * LANES], turned, (((0,), (0,)), ((), ())),
            preferred_element_type=F32,
        ).astype(BF16)
        for k in range(LANES // d):
            x_out[c * (LANES // d) + k] = part[k * d:(k + 1) * d]


def pack(starts, spare, x_ref, plain, rows, weights, parts):
    blocks, d, _ = x_ref.shape
    lane = lax.broadcasted_iota(jnp.int32, (d, TILE), 1)
    fill = jnp.zeros((LANES - parts * d, TILE), BF16)
    for c in range(LIVE // TILE):
        v = None
        for b in range(c, min(blocks, c + spare + 1)):
            piece = x_ref[b].astype(F32)
            v = piece if v is None else jnp.where(lane >= starts[b] - c * TILE, piece, v)
        if plain is not None:
            plain[c] = v.astype(BF16)
        rows[c] = jnp.concatenate([v] * (LANES // d), axis=0).T.astype(BF16)
        split = pieces(v * (d ** -0.5 * LOG2E), parts)
        weights[c] = jnp.concatenate(split + [fill] if parts * d < LANES else split, axis=0)


def step(later, now, diagonal, rows, weights, into, source, tops, running, state, keep, other):
    now_at = [tile_of(*c) for c in now]
    now_top = [tops[here] for here in now_at]
    sums = [[jnp.zeros(tops.shape[1:], F32)] * 2 for _ in now]
    made = [jnp.dot(rows[j], weights[i], preferred_element_type=F32) for i, j in later]
    tallest = [None for _ in later]
    for u in range(max(len(now), len(later))):
        for g in range(TILE // 8):
            if now:
                v = source[u, g]
                p = jnp.exp2(v - now_top[u])
                sums[u] = [sums[u][0] + p, sums[u][1]]
                if other is None:
                    keep[now_at[u], g] = v
                else:
                    keep[now_at[u], g] = p
                    sums[u][1] = sums[u][1] + p * (v - other[now_at[u], g])
            if later:
                v = made[u][g * 8:(g + 1) * 8]
                if diagonal:
                    row = lax.broadcasted_iota(jnp.int32, v.shape, 0) + g * 8
                    v = jnp.where(row <= lax.broadcasted_iota(jnp.int32, v.shape, 1), v, NEGATIVE)
                into[u, g] = v
                tallest[u] = v if g == 0 else jnp.maximum(tallest[u], v)
    for u, (i, j) in enumerate(later):
        top = jnp.maximum(tallest[u], running[i])
        running[i] = top
        tops[tile_of(i, j)] = top
    for u, (i, _) in enumerate(now):
        less = jnp.exp2(state[i, 0] - now_top[u])
        state[i, 0] = now_top[u]
        state[i, 1] = state[i, 1] * less + sums[u][0]
        if other is not None:
            state[i, 2] = state[i, 2] * less + sums[u][1]


def by_parity(count, even, odd, run):
    @pl.when((count & 1) == 0)
    def _():
        run(even, odd)

    @pl.when((count & 1) == 1)
    def _():
        run(odd, even)


def chain(first, after, count):
    out = [first]
    while len(out) < count:
        out.append(after(*out[-1]))
    return out


def sweep(unit, rows, weights, even, odd, tops, running, state, keep, other):
    blocks = rows.shape[0]
    running[...] = jnp.full(running.shape, NEGATIVE, F32)
    state[:, :1] = jnp.full((blocks, 1, *running.shape[1:]), NEGATIVE, F32)
    state[:, 1:] = jnp.zeros((blocks, state.shape[1] - 1, *running.shape[1:]), F32)

    def run(first, after, tiles, diagonal):
        def one(later, now, into, source):
            step(
                later, now, diagonal, rows, weights, into, source, tops, running, state, keep,
                other,
            )

        def trip(count, now):
            later = chain(after(*now[-1]), after, unit)
            by_parity(count, even, odd, lambda source, into: one(later, now, into, source))
            return later

        now = chain((jnp.int32(first[0]), jnp.int32(first[1])), after, unit)
        one(now, [], even, None)
        trips = tiles // unit - 1
        now = lax.fori_loop(0, trips, trip, now)
        one([], now, None, odd if trips % 2 else even)

    def below(i, j):
        wrap = j + 1 == i
        return jnp.where(wrap, i + 1, i), jnp.where(wrap, 0, j + 1)

    run((0, 0), lambda i, j: (i + 1, j + 1), blocks, True)
    run((1, 0), below, blocks * (blocks - 1) // 2, False)


def totals(s_state, t_state, stats):
    def collect(state):
        top8 = state[:, 0]
        top = jnp.max(top8, axis=1, keepdims=True)
        less = jnp.exp2(top8 - top)
        return top, [
            jnp.sum(state[:, k] * less, axis=1, keepdims=True) for k in range(1, state.shape[1])
        ]

    s_top, (s_sum,) = collect(s_state)
    t_top, (t_sum, cross) = collect(t_state)
    s_lse = s_top + jnp.log2(s_sum)
    kl = cross / t_sum - (t_top + jnp.log2(t_sum)) + s_lse
    stats[...] = jnp.concatenate([s_lse, t_top, 1.0 / t_sum, s_lse], axis=1)
    return jnp.sum(kl, axis=0) * LN2


def back(i, j):
    wrap = j == i
    return jnp.where(wrap, i - 1, i), jnp.where(wrap, 0, j + 1)


def gradient_step(later, now, into, source, students, s_ref, pt_ref, tops, stats, grad):
    nt = (((1,), (1,)), ((), ()))
    parts = [
        (
            lax.dot_general(students[i], source[u], nt, preferred_element_type=F32),
            jnp.dot(students[j], source[u], preferred_element_type=F32),
        )
        for u, (i, j) in enumerate(now)
    ]
    for u, (i, j) in enumerate(later):
        here = tile_of(i, j)
        s_lse, t_top, t_inv = (stats[i, pl.ds(k, 1), :] for k in range(3))
        t_scale = jnp.exp2(tops[here] - t_top) * t_inv
        for g in range(0, TILE // 8, 2):
            w = jnp.exp2(s_ref[here, g:g + 2] - s_lse) - pt_ref[here, g:g + 2] * t_scale
            into[u, g * 8:g * 8 + 16, :] = w.reshape(16, TILE).astype(BF16)
    for (i, j), (key_grad, query_grad) in zip(now, parts):
        grad[j] += key_grad
        grad[i] += query_grad


def gradients(first, last, final, now, even, odd, row_done, *refs):
    def one(later, now, into, source):
        gradient_step(later, now, into, source, *refs)

    def check(now):
        for i, j in now:
            pl.when(i == j)(functools.partial(row_done, i))

    def trip(count, now):
        later = chain(back(*now[-1]), back, len(now))
        by_parity(count, even, odd, lambda source, into: one(later, now, into, source))
        check(now)
        return later

    now = lax.fori_loop(first, last - final, trip, now)
    if final:
        one([], now, None, odd if (last - 1) % 2 else even)
        check(now)
    return now


def compute_scratch(dt, ds):
    blocks = LIVE // TILE
    tiles = blocks * (blocks + 1) // 2
    groups = TILE // 8
    wide = max(STUDENT_TILES, TEACHER_TILES)
    return dict(
        students=pltpu.VMEM((blocks, ds, TILE), BF16),
        rows=pltpu.VMEM((2, blocks, TILE, LANES), BF16),
        weights=pltpu.VMEM((2, blocks, LANES, TILE), BF16),
        even=pltpu.VMEM((wide, groups, 8, TILE), F32),
        odd=pltpu.VMEM((wide, groups, 8, TILE), F32),
        s_ref=pltpu.VMEM((tiles, groups, 8, TILE), F32),
        pt_ref=pltpu.VMEM((tiles, groups, 8, TILE), F32),
        tops=pltpu.VMEM((tiles, 8, TILE), F32),
        running=pltpu.VMEM((blocks, 8, TILE), F32),
        s_state=pltpu.VMEM((blocks, 2, 8, TILE), F32),
        t_state=pltpu.VMEM((blocks, 3, 8, TILE), F32),
        stats=pltpu.VMEM((blocks, 4, TILE), F32),
        w_even=pltpu.VMEM((GRADIENT_TILES, TILE, TILE), BF16),
        w_odd=pltpu.VMEM((GRADIENT_TILES, TILE, TILE), BF16),
        grad=pltpu.VMEM((blocks, ds, TILE), F32),
    )


def student_phase(starts, spare, x_in, c):
    pack(starts, spare, x_in, c["students"], c["rows"].at[0], c["weights"].at[0], 3)
    sweep(
        STUDENT_TILES, c["rows"].at[0], c["weights"].at[0], c["even"], c["odd"], c["tops"],
        c["running"], c["s_state"], c["s_ref"], None,
    )


def teacher_phase(starts, spare, x_in, c):
    pack(starts, spare, x_in, None, c["rows"].at[1], c["weights"].at[1], 2)
    sweep(
        TEACHER_TILES, c["rows"].at[1], c["weights"].at[1], c["even"], c["odd"], c["tops"],
        c["running"], c["t_state"], c["pt_ref"], c["s_ref"],
    )
    return totals(c["s_state"], c["t_state"], c["stats"])


def gradient_phase(first, last, final, now, c, row_done):
    refs = [c[k] for k in ("students", "s_ref", "pt_ref", "tops", "stats", "grad")]
    if now is None:
        now = chain((jnp.int32(LIVE // TILE - 1), jnp.int32(0)), back, GRADIENT_TILES)
        gradient_step(now, [], c["w_even"], None, *refs)
    return gradients(first, last, final, now, c["w_even"], c["w_odd"], row_done, *refs)


def kernel(
    n, m, counts, t_ref, s_ref, o_ref, loss_ref,
    t_out, s_out, t_in, s_in, c, g_out, g_in, starts, part, row, grid, sems,
):
    x_send, x_recv, g_send, g_recv, seq_send, seq_recv, head_send, head_recv, own = sems
    blocks = LIVE // TILE
    spare = n - blocks
    grad = c["grad"]
    ds = grad.shape[1]
    me, peers = others("seq", n)
    my_head, head_peers = others("head", m)
    barrier = pltpu.get_barrier_semaphore()
    for peer in [{"seq": p} for p in peers] + [{"head": p} for p in head_peers]:
        pl.semaphore_signal(barrier, inc=1, device_id=peer, device_id_type=MESH)

    shift, real = own_start(counts, n)
    turned = turn(shift, TILE)
    enter(s_ref, turned, s_out)
    enter(t_ref, turned, t_out)
    start = jnp.int32(0)
    scalars = []
    for b in range(n):
        starts[b] = start
        scalars.append(start)
        start = start + counts[b]
    grad[...] = jnp.zeros_like(grad)
    pl.semaphore_wait(barrier, n - 1 + m - 1)

    copies = []
    for kind, (src, dst) in enumerate(((s_out, s_in), (t_out, t_in))):
        keep = pltpu.make_async_copy(src.at[me], dst.at[me], own.at[kind])
        keep.start()
        copies.append([
            send(src.at[p], dst.at[me], x_send.at[kind, k], x_recv.at[kind, k], {"seq": p})
            for k, p in enumerate(peers)
        ] + [keep])
    for copy in copies[0]:
        copy.wait()
    student_phase(scalars, spare, s_in, c)
    for copy in copies[1]:
        copy.wait()
    loss = teacher_phase(scalars, spare, t_in, c)
    part[...] = loss[:, :LANES] + loss[:, LANES:]

    def finish_block(b):
        lane = lax.broadcasted_iota(jnp.int32, grad.shape[1:], 1)
        first = starts[b]
        top = blocks - 1
        v = grad[jnp.minimum(b, top)]
        for k in range(1, spare + 1):
            q = jnp.clip(b - k, 0, top)
            v = jnp.where(lane + q * TILE >= first, grad[q], v)
        g_out[b] = v.astype(BF16)

    def to_owner(b):
        @pl.when(b == me)
        def _():
            pltpu.make_async_copy(g_out.at[b], g_in.at[me], own.at[1]).start()

        @pl.when(b != me)
        def _():
            send(g_out.at[b], g_in.at[me], g_send.at[b], g_recv.at[me], {"seq": b})

    def row_done(i):
        @pl.when(i + spare + 1 < n)
        def _():
            to_owner(i + spare + 1)

        finish_block(i + spare)

    trips = blocks * (blocks + 1) // 2 // GRADIENT_TILES
    now = gradient_phase(0, 1, False, None, c, row_done)
    own_part = pltpu.make_async_copy(part, row.at[me], own.at[0])
    own_part.start()
    parts = [
        send(part, row.at[me], seq_send.at[k], seq_recv.at[k], {"seq": p})
        for k, p in enumerate(peers)
    ]
    now = gradient_phase(1, trips - 2, False, now, c, row_done)
    own_part.wait()
    for copy in parts:
        copy.wait()
    own_row = pltpu.make_async_copy(row, grid.at[my_head], own.at[0])
    own_row.start()
    row_copies = [
        send(row, grid.at[my_head], head_send.at[k], head_recv.at[k], {"head": p})
        for k, p in enumerate(head_peers)
    ]
    gradient_phase(trips - 2, trips, True, now, c, row_done)
    for b in range(spare):
        finish_block(b)
    for b in range(spare, -1, -1):
        to_owner(b)
    own_row.wait()
    for copy in row_copies:
        copy.wait()
    whole = jnp.int32(0)
    for b in range(n):
        whole = whole + counts[b]
    loss_ref[...] = jnp.sum(jnp.sum(grid[...], axis=(0, 1)), axis=1, keepdims=True) / (
        H_REL * whole.astype(F32)
    )
    unturned = turn(shift, real)
    pltpu.make_async_copy(g_out.at[me], g_in.at[me], own.at[1]).wait()
    for p in peers:
        pltpu.make_async_remote_copy(
            src_ref=g_out.at[p], dst_ref=g_in.at[p], send_sem=g_send.at[p],
            recv_sem=g_recv.at[p], device_id={"seq": p}, device_id_type=MESH,
        ).wait()
    per = TILE // ds
    for k in range(n // per):
        o_ref[:, k * TILE:(k + 1) * TILE] = ds ** -0.5 * lax.dot_general(
            unturned, g_in[k * per:(k + 1) * per].reshape(TILE, TILE),
            (((1,), (1,)), ((), ())), preferred_element_type=F32,
        )


def local(teacher, student, counts):
    n, m = lax.axis_size("seq"), lax.axis_size("head")
    tokens = teacher.shape[0]
    dt, ds = teacher.shape[1] // n, student.shape[1] // n
    vmem = pl.BlockSpec(memory_space=pltpu.VMEM)
    dma = pltpu.SemaphoreType.DMA
    grad, loss = pl.pallas_call(
        functools.partial(kernel, n, m),
        out_shape=(
            jax.ShapeDtypeStruct((tokens, n * ds), F32),
            jax.ShapeDtypeStruct((1, 1), F32),
        ),
        in_specs=[pl.BlockSpec(memory_space=pltpu.SMEM), vmem, vmem],
        out_specs=(vmem, vmem),
        scratch_shapes=[
            pltpu.VMEM((n, dt, tokens), BF16),
            pltpu.VMEM((n, ds, tokens), BF16),
            pltpu.VMEM((n, dt, tokens), BF16),
            pltpu.VMEM((n, ds, tokens), BF16),
            compute_scratch(dt, ds),
            pltpu.VMEM((n, ds, tokens), BF16),
            pltpu.VMEM((n, ds, tokens), BF16),
            pltpu.SMEM((n,), jnp.int32),
            pltpu.VMEM((1, LANES), F32),
            pltpu.VMEM((n, 1, LANES), F32),
            pltpu.VMEM((m, n, 1, LANES), F32),
            [dma((2, n - 1))] * 2 + [dma((n,))] * 2 + [dma((n - 1,))] * 2
            + [dma((m - 1,))] * 2 + [dma((2,))],
        ],
        compiler_params=pltpu.CompilerParams(
            collective_id=0, has_side_effects=True, vmem_limit_bytes=62 << 20
        ),
    )(counts, teacher, student)
    return grad, loss.reshape(())


def solution(mesh):
    return jax.shard_map(
        local,
        mesh=mesh,
        in_specs=(P("seq", "head"), P("seq", "head"), P()),
        out_specs=(P("seq", "head"), P()),
        check_vma=False,
    )
```

time: 60.8 us -> 53.7 us (0.88)
  Pallas kernels: 60 us -> 49.3 us
  local copies, waits for them, and re-layouts: 0 us -> 1.87 us
  between operations: 0.64 us -> 2.34 us
    pallas_call x3 -> x1, Pallas kernels: 60 us -> 49.3 us  [local(): pl.pallas_call(functools.partial(kernel, n, m), out_shape=(jax.ShapeDtype...]
    unnamed x0 -> x1, local copies, waits for them, and re-layouts: none -> 1.87 us
where the time goes in v4:
time: 53.7 us; the launch traced here: 53.5 us
  Pallas kernels  49.3 us (92%)
  between operations  2.34 us (4%)
  local copies, waits for them, and re-layouts  1.87 us (3%)
    pallas_call x1, Pallas kernels, local(): pl.pallas_call(functools.partial(kernel, n, m), out_shape=(jax.ShapeDtype...  49.3 us
    unnamed x1, local copies, waits for them, and re-layouts  1.87 us

profile of v4, /device:TPU:1, one launch (start us, length us, event | category | flops | bytes accessed | tf_op | source)
XLA Modules:
  0.0 53.5 jit_solution(12972549985818037972)
XLA Ops:
  0.6 49.3 %shard_map.50 = (f32[256,512]{1,0:T(8,128)}, f32[1,1]{1,0:T(1,128)}) custom-call(s32[16]{0:T(128)} %counts.1, bf16[256,1024]{1,0:T(8,128)(2,1)} %t_ref.1, bf16[256,512]{1,0:T(8,128)(2,1)} %s_ref.1), custom_call_target="tpu_custom_call" | custom-call | tf_op jit(solution)/shard_map/pallas_call | solution.py:415
  49.9 1.9 %copy.7 = f32[256,512]{1,0:T(8,128)} copy(f32[256,512]{1,0:T(8,128)} %get-tuple-element.8) | data formatting | bytes 1048576

commit v5 on v4

--- a/solution.py
+++ b/solution.py
@@ -9,9 +9,9 @@
 
 H_REL = 128
 LIVE = 3072
-STUDENT_TILES = 6
-TEACHER_TILES = 6
-GRADIENT_TILES = 6
+DIAGONAL_TILES = 12
+LOWER_TILES = 11
+GRADIENT_TILES = 13
 TILE = 256
 LANES = 128
 LOG2E = 1.4426950408889634
@@ -25,6 +25,18 @@
 def others(axis, n):
     me = lax.axis_index(axis)
     return me, [lax.rem(me + k, n) for k in range(1, n)]
+
+
+def far_first(ring):
+    me = lax.axis_index("seq")
+    y, z, core = lax.div(me, 4), lax.div(me, 2) & 1, me & 1
+    offsets = [(dy, dz, dc) for dy in range(ring) for dz in range(2) for dc in range(2)]
+    offsets.sort(key=lambda o: (-min(o[0], ring - o[0]) - 2 * o[1], o))
+    return me, [
+        lax.rem(y + dy, ring) * 4 + ((z + dz) & 1) * 2 + ((core + dc) & 1)
+        for dy, dz, dc in offsets
+        if dy + dz + dc
+    ]
 
 
 def send(src, dst, send_sem, recv_sem, device):
@@ -95,9 +107,12 @@
     now_at = [tile_of(*c) for c in now]
     now_top = [tops[here] for here in now_at]
     sums = [[jnp.zeros(tops.shape[1:], F32)] * 2 for _ in now]
-    made = [jnp.dot(rows[j], weights[i], preferred_element_type=F32) for i, j in later]
+    made = []
     tallest = [None for _ in later]
     for u in range(max(len(now), len(later))):
+        if later:
+            i, j = later[u]
+            made.append(jnp.dot(rows[j], weights[i], preferred_element_type=F32))
         for g in range(TILE // 8):
             if now:
                 v = source[u, g]
@@ -144,13 +159,13 @@
     return out
 
 
-def sweep(unit, rows, weights, even, odd, tops, running, state, keep, other):
+def sweep(rows, weights, even, odd, tops, running, state, keep, other):
     blocks = rows.shape[0]
     running[...] = jnp.full(running.shape, NEGATIVE, F32)
     state[:, :1] = jnp.full((blocks, 1, *running.shape[1:]), NEGATIVE, F32)
     state[:, 1:] = jnp.zeros((blocks, state.shape[1] - 1, *running.shape[1:]), F32)
 
-    def run(first, after, tiles, diagonal):
+    def run(first, after, tiles, unit, diagonal):
         def one(later, now, into, source):
             step(
                 later, now, diagonal, rows, weights, into, source, tops, running, state, keep,
@@ -165,15 +180,20 @@
         now = chain((jnp.int32(first[0]), jnp.int32(first[1])), after, unit)
         one(now, [], even, None)
         trips = tiles // unit - 1
-        now = lax.fori_loop(0, trips, trip, now)
+        if trips == 1:
+            later = chain(after(*now[-1]), after, unit)
+            one(later, now, odd, even)
+            now = later
+        else:
+            now = lax.fori_loop(0, trips, trip, now)
         one([], now, None, odd if trips % 2 else even)
 
     def below(i, j):
         wrap = j + 1 == i
         return jnp.where(wrap, i + 1, i), jnp.where(wrap, 0, j + 1)
 
-    run((0, 0), lambda i, j: (i + 1, j + 1), blocks, True)
-    run((1, 0), below, blocks * (blocks - 1) // 2, False)
+    run((0, 0), lambda i, j: (i + 1, j + 1), blocks, DIAGONAL_TILES, True)
+    run((1, 0), below, blocks * (blocks - 1) // 2, LOWER_TILES, False)
 
 
 def totals(s_state, t_state, stats):
@@ -200,14 +220,17 @@
 
 def gradient_step(later, now, into, source, students, s_ref, pt_ref, tops, stats, grad):
     nt = (((1,), (1,)), ((), ()))
-    parts = [
-        (
-            lax.dot_general(students[i], source[u], nt, preferred_element_type=F32),
-            jnp.dot(students[j], source[u], preferred_element_type=F32),
-        )
-        for u, (i, j) in enumerate(now)
-    ]
-    for u, (i, j) in enumerate(later):
+    parts = []
+    for u in range(max(len(now), len(later))):
+        if now:
+            i, j = now[u]
+            parts.append((
+                lax.dot_general(students[i], source[u], nt, preferred_element_type=F32),
+                jnp.dot(students[j], source[u], preferred_element_type=F32),
+            ))
+        if not later:
+            continue
+        i, j = later[u]
         here = tile_of(i, j)
         s_lse, t_top, t_inv = (stats[i, pl.ds(k, 1), :] for k in range(3))
         t_scale = jnp.exp2(tops[here] - t_top) * t_inv
@@ -244,7 +267,7 @@
     blocks = LIVE // TILE
     tiles = blocks * (blocks + 1) // 2
     groups = TILE // 8
-    wide = max(STUDENT_TILES, TEACHER_TILES)
+    wide = max(DIAGONAL_TILES, LOWER_TILES)
     return dict(
         students=pltpu.VMEM((blocks, ds, TILE), BF16),
         rows=pltpu.VMEM((2, blocks, TILE, LANES), BF16),
@@ -267,7 +290,7 @@
 def student_phase(starts, spare, x_in, c):
     pack(starts, spare, x_in, c["students"], c["rows"].at[0], c["weights"].at[0], 3)
     sweep(
-        STUDENT_TILES, c["rows"].at[0], c["weights"].at[0], c["even"], c["odd"], c["tops"],
+        c["rows"].at[0], c["weights"].at[0], c["even"], c["odd"], c["tops"],
         c["running"], c["s_state"], c["s_ref"], None,
     )
 
@@ -275,7 +298,7 @@
 def teacher_phase(starts, spare, x_in, c):
     pack(starts, spare, x_in, None, c["rows"].at[1], c["weights"].at[1], 2)
     sweep(
-        TEACHER_TILES, c["rows"].at[1], c["weights"].at[1], c["even"], c["odd"], c["tops"],
+        c["rows"].at[1], c["weights"].at[1], c["even"], c["odd"], c["tops"],
         c["running"], c["t_state"], c["pt_ref"], c["s_ref"],
     )
     return totals(c["s_state"], c["t_state"], c["stats"])
@@ -291,23 +314,29 @@
 
 def kernel(
     n, m, counts, t_ref, s_ref, o_ref, loss_ref,
-    t_out, s_out, t_in, s_in, c, g_out, g_in, starts, part, row, grid, sems,
+    t_own, s_own, t_out, s_out, t_in, s_in, c, g_out, g_in, starts, part, row, grid, sems,
 ):
     x_send, x_recv, g_send, g_recv, seq_send, seq_recv, head_send, head_recv, own = sems
     blocks = LIVE // TILE
     spare = n - blocks
     grad = c["grad"]
     ds = grad.shape[1]
-    me, peers = others("seq", n)
+    me, peers = far_first(n // 4)
     my_head, head_peers = others("head", m)
     barrier = pltpu.get_barrier_semaphore()
     for peer in [{"seq": p} for p in peers] + [{"head": p} for p in head_peers]:
         pl.semaphore_signal(barrier, inc=1, device_id=peer, device_id_type=MESH)
 
+    s_load = pltpu.make_async_copy(s_ref, s_own, own.at[0])
+    t_load = pltpu.make_async_copy(t_ref, t_own, own.at[1])
+    s_load.start()
+    t_load.start()
     shift, real = own_start(counts, n)
     turned = turn(shift, TILE)
-    enter(s_ref, turned, s_out)
-    enter(t_ref, turned, t_out)
+    s_load.wait()
+    enter(s_own, turned, s_out)
+    t_load.wait()
+    enter(t_own, turned, t_out)
     start = jnp.int32(0)
     scalars = []
     for b in range(n):
@@ -367,7 +396,7 @@
         send(part, row.at[me], seq_send.at[k], seq_recv.at[k], {"seq": p})
         for k, p in enumerate(peers)
     ]
-    now = gradient_phase(1, trips - 2, False, now, c, row_done)
+    now = gradient_phase(1, trips - 1, False, now, c, row_done)
     own_part.wait()
     for copy in parts:
         copy.wait()
@@ -377,7 +406,7 @@
         send(row, grid.at[my_head], head_send.at[k], head_recv.at[k], {"head": p})
         for k, p in enumerate(head_peers)
     ]
-    gradient_phase(trips - 2, trips, True, now, c, row_done)
+    gradient_phase(trips - 1, trips, True, now, c, row_done)
     for b in range(spare):
         finish_block(b)
     for b in range(spare, -1, -1):
@@ -400,10 +429,10 @@
         ).wait()
     per = TILE // ds
     for k in range(n // per):
-        o_ref[:, k * TILE:(k + 1) * TILE] = ds ** -0.5 * lax.dot_general(
+        o_ref[:, k * TILE:(k + 1) * TILE] = lax.dot_general(
             unturned, g_in[k * per:(k + 1) * per].reshape(TILE, TILE),
             (((1,), (1,)), ((), ())), preferred_element_type=F32,
-        )
+        ).astype(BF16)
 
 
 def local(teacher, student, counts):
@@ -411,16 +440,19 @@
     tokens = teacher.shape[0]
     dt, ds = teacher.shape[1] // n, student.shape[1] // n
     vmem = pl.BlockSpec(memory_space=pltpu.VMEM)
+    any_space = pl.BlockSpec(memory_space=pl.ANY)
     dma = pltpu.SemaphoreType.DMA
     grad, loss = pl.pallas_call(
         functools.partial(kernel, n, m),
         out_shape=(
-            jax.ShapeDtypeStruct((tokens, n * ds), F32),
+            jax.ShapeDtypeStruct((tokens, n * ds), BF16),
             jax.ShapeDtypeStruct((1, 1), F32),
         ),
-        in_specs=[pl.BlockSpec(memory_space=pltpu.SMEM), vmem, vmem],
+        in_specs=[pl.BlockSpec(memory_space=pltpu.SMEM), any_space, any_space],
         out_specs=(vmem, vmem),
         scratch_shapes=[
+            pltpu.VMEM(teacher.shape, BF16),
+            pltpu.VMEM(student.shape, BF16),
             pltpu.VMEM((n, dt, tokens), BF16),
             pltpu.VMEM((n, ds, tokens), BF16),
             pltpu.VMEM((n, dt, tokens), BF16),
@@ -439,7 +471,7 @@
             collective_id=0, has_side_effects=True, vmem_limit_bytes=62 << 20
         ),
     )(counts, teacher, student)
-    return grad, loss.reshape(())
+    return grad.astype(F32) * ds ** -0.5, loss.reshape(())
 
 
 def solution(mesh):

time: 53.7 us -> 51.7 us (0.963)
  Pallas kernels: 49.3 us -> 47.3 us
  local copies, waits for them, and re-layouts: 1.87 us -> 0 us
  other arithmetic: 0 us -> 1.81 us
    pallas_call x1, Pallas kernels: 49.3 us -> 47.3 us  [local(): pl.pallas_call(functools.partial(kernel, n, m), out_shape=(jax.ShapeDtype...]
    unnamed x1 -> x0, local copies, waits for them, and re-layouts: 1.87 us -> none
    mul x0 -> x1, other arithmetic: none -> 1.81 us  [local(): return (grad.astype(F32) * ds ** (-0.5), loss.reshape(()))]
where the time goes in v5:
time: 51.7 us; the launch traced here: 51.5 us
  Pallas kernels  47.3 us (91%)
  between operations  2.4 us (5%)
  other arithmetic  1.81 us (4%)
    pallas_call x1, Pallas kernels, local(): pl.pallas_call(functools.partial(kernel, n, m), out_shape=(jax.ShapeDtype...  47.3 us
    mul x1, other arithmetic, local(): return (grad.astype(F32) * ds ** (-0.5), loss.reshape(()))  1.81 us

profile of v5, /device:TPU:1, one launch (start us, length us, event | category | flops | bytes accessed | tf_op | source)
XLA Modules:
  0.0 51.5 jit_solution(14259214972530587073)
XLA Ops:
  0.6 47.3 %shard_map.50 = (bf16[256,512]{1,0:T(8,128)(2,1)}, f32[1,1]{1,0:T(1,128)}) custom-call(s32[16]{0:T(128)} %counts.1, bf16[256,1024]{1,0:T(8,128)(2,1)} %t_ref.1, bf16[256,512]{1,0:T(8,128)(2,1)} %s_ref.1), custom_call_target="tpu_custom_call" | custom-call | tf_op jit(solution)/shard_map/pallas_call | solution.py:445
  47.9 1.8 %convert_multiply_fusion = f32[256,512]{1,0:T(8,128)} fusion(bf16[256,512]{1,0:T(8,128)(2,1)} %get-tuple-element.4), kind=kLoop, calls=%fused_computation | loop fusion | flops 262144 | bytes 786432 | tf_op jit(solution)/shard_map/mul | solution.py:474

commit v6 on v5

--- a/solution.py
+++ b/solution.py
@@ -313,8 +313,8 @@
 
 
 def kernel(
-    n, m, counts, t_ref, s_ref, o_ref, loss_ref,
-    t_own, s_own, t_out, s_out, t_in, s_in, c, g_out, g_in, starts, part, row, grid, sems,
+    n, m, counts, t_ref, s_ref, g_in, loss_ref,
+    t_own, s_own, t_out, s_out, t_in, s_in, c, g_out, starts, part, row, grid, sems,
 ):
     x_send, x_recv, g_send, g_recv, seq_send, seq_recv, head_send, head_recv, own = sems
     blocks = LIVE // TILE
@@ -331,7 +331,7 @@
     t_load = pltpu.make_async_copy(t_ref, t_own, own.at[1])
     s_load.start()
     t_load.start()
-    shift, real = own_start(counts, n)
+    shift, _ = own_start(counts, n)
     turned = turn(shift, TILE)
     s_load.wait()
     enter(s_own, turned, s_out)
@@ -389,14 +389,14 @@
         finish_block(i + spare)
 
     trips = blocks * (blocks + 1) // 2 // GRADIENT_TILES
-    now = gradient_phase(0, 1, False, None, c, row_done)
+    now = gradient_phase(0, 0, False, None, c, row_done)
     own_part = pltpu.make_async_copy(part, row.at[me], own.at[0])
     own_part.start()
     parts = [
         send(part, row.at[me], seq_send.at[k], seq_recv.at[k], {"seq": p})
         for k, p in enumerate(peers)
     ]
-    now = gradient_phase(1, trips - 1, False, now, c, row_done)
+    now = gradient_phase(0, trips - 1, False, now, c, row_done)
     own_part.wait()
     for copy in parts:
         copy.wait()
@@ -420,19 +420,23 @@
     loss_ref[...] = jnp.sum(jnp.sum(grid[...], axis=(0, 1)), axis=1, keepdims=True) / (
         H_REL * whole.astype(F32)
     )
-    unturned = turn(shift, real)
     pltpu.make_async_copy(g_out.at[me], g_in.at[me], own.at[1]).wait()
     for p in peers:
         pltpu.make_async_remote_copy(
             src_ref=g_out.at[p], dst_ref=g_in.at[p], send_sem=g_send.at[p],
             recv_sem=g_recv.at[p], device_id={"seq": p}, device_id_type=MESH,
         ).wait()
+
+
+def leave_kernel(n, counts, g_ref, o_ref):
+    ds = g_ref.shape[1]
     per = TILE // ds
+    turned = turn(*own_start(counts, n))
     for k in range(n // per):
-        o_ref[:, k * TILE:(k + 1) * TILE] = lax.dot_general(
-            unturned, g_in[k * per:(k + 1) * per].reshape(TILE, TILE),
+        o_ref[:, k * TILE:(k + 1) * TILE] = ds ** -0.5 * lax.dot_general(
+            turned, g_ref[k * per:(k + 1) * per].reshape(TILE, TILE),
             (((1,), (1,)), ((), ())), preferred_element_type=F32,
-        ).astype(BF16)
+        )
 
 
 def local(teacher, student, counts):
@@ -441,15 +445,16 @@
     dt, ds = teacher.shape[1] // n, student.shape[1] // n
     vmem = pl.BlockSpec(memory_space=pltpu.VMEM)
     any_space = pl.BlockSpec(memory_space=pl.ANY)
+    smem = pl.BlockSpec(memory_space=pltpu.SMEM)
     dma = pltpu.SemaphoreType.DMA
     grad, loss = pl.pallas_call(
         functools.partial(kernel, n, m),
         out_shape=(
-            jax.ShapeDtypeStruct((tokens, n * ds), BF16),
+            jax.ShapeDtypeStruct((n, ds, tokens), BF16),
             jax.ShapeDtypeStruct((1, 1), F32),
         ),
-        in_specs=[pl.BlockSpec(memory_space=pltpu.SMEM), any_space, any_space],
-        out_specs=(vmem, vmem),
+        in_specs=[smem, any_space, any_space],
+        out_specs=(any_space, vmem),
         scratch_shapes=[
             pltpu.VMEM(teacher.shape, BF16),
             pltpu.VMEM(student.shape, BF16),
@@ -458,7 +463,6 @@
             pltpu.VMEM((n, dt, tokens), BF16),
             pltpu.VMEM((n, ds, tokens), BF16),
             compute_scratch(dt, ds),
-            pltpu.VMEM((n, ds, tokens), BF16),
             pltpu.VMEM((n, ds, tokens), BF16),
             pltpu.SMEM((n,), jnp.int32),
             pltpu.VMEM((1, LANES), F32),
@@ -471,7 +475,13 @@
             collective_id=0, has_side_effects=True, vmem_limit_bytes=62 << 20
         ),
     )(counts, teacher, student)
-    return grad.astype(F32) * ds ** -0.5, loss.reshape(())
+    grad = pl.pallas_call(
+        functools.partial(leave_kernel, n),
+        out_shape=jax.ShapeDtypeStruct((tokens, n * ds), F32),
+        in_specs=[smem, vmem],
+        out_specs=vmem,
+    )(counts, grad)
+    return grad, loss.reshape(())
 
 
 def solution(mesh):

time: 51.7 us -> 51.1 us (0.988)
  other arithmetic: 1.81 us -> 0 us
  Pallas kernels: 47.3 us -> 48.5 us
    pallas_call x0 -> x1, Pallas kernels: none -> 2.02 us  [local(): pl.pallas_call(functools.partial(leave_kernel, n), out_shape=jax.ShapeDty...]
    mul x1 -> x0, other arithmetic: 1.81 us -> none  [local(): return (grad.astype(F32) * ds ** (-0.5), loss.reshape(()))]
    pallas_call x1, Pallas kernels: 47.3 us -> 46.5 us  [local(): pl.pallas_call(functools.partial(kernel, n, m), out_shape=(jax.ShapeDtype...]
where the time goes in v6:
time: 51.1 us; the launch traced here: 50.9 us
  Pallas kernels  48.5 us (95%)
  between operations  2.4 us (5%)
    pallas_call x1, Pallas kernels, local(): pl.pallas_call(functools.partial(kernel, n, m), out_shape=(jax.ShapeDtype...  46.5 us
    pallas_call x1, Pallas kernels, local(): pl.pallas_call(functools.partial(leave_kernel, n), out_shape=jax.ShapeDty...  2.02 us

profile of v6, /device:TPU:1, one launch (start us, length us, event | category | flops | bytes accessed | tf_op | source)
XLA Modules:
  0.0 50.9 jit_solution(3160494737166671265)
XLA Ops:
  0.6 46.5 %shard_map.50 = (bf16[16,32,256]{2,1,0:T(8,128)(2,1)}, f32[1,1]{1,0:T(1,128)}) custom-call(s32[16]{0:T(128)} %counts.3, bf16[256,1024]{1,0:T(8,128)(2,1)} %t_ref.1, bf16[256,512]{1,0:T(8,128)(2,1)} %s_ref.1), custom_call_target="tpu_custom_call" | custom-call | tf_op jit(solution)/shard_map/pallas_call | solution.py:450
  47.1 2.0 %shard_map.51 = f32[256,512]{1,0:T(8,128)} custom-call(s32[16]{0:T(128)} %counts.3, bf16[16,32,256]{2,1,0:T(8,128)(2,1)} %get-tuple-element.4.g_ref), custom_call_target="tpu_custom_call" | custom-call | tf_op jit(solution)/shard_map/pallas_call | solution.py:478

commit v7 on v6

--- a/solution.py
+++ b/solution.py
@@ -346,17 +346,21 @@
     grad[...] = jnp.zeros_like(grad)
     pl.semaphore_wait(barrier, n - 1 + m - 1)
 
-    copies = []
+    copies, keeps = [], []
     for kind, (src, dst) in enumerate(((s_out, s_in), (t_out, t_in))):
-        keep = pltpu.make_async_copy(src.at[me], dst.at[me], own.at[kind])
-        keep.start()
+        for copy in copies[0] if kind else []:
+            copy.wait_send()
+        keeps.append(pltpu.make_async_copy(src.at[me], dst.at[me], own.at[kind]))
+        keeps[kind].start()
         copies.append([
             send(src.at[p], dst.at[me], x_send.at[kind, k], x_recv.at[kind, k], {"seq": p})
             for k, p in enumerate(peers)
-        ] + [keep])
+        ])
+    keeps[0].wait()
     for copy in copies[0]:
-        copy.wait()
+        copy.wait_recv()
     student_phase(scalars, spare, s_in, c)
+    keeps[1].wait()
     for copy in copies[1]:
         copy.wait()
     loss = teacher_phase(scalars, spare, t_in, c)

time: 51.1 us -> 48.9 us (0.957)
  Pallas kernels: 48.5 us -> 46.3 us
    pallas_call x1, Pallas kernels: 46.5 us -> 44.3 us  [local(): pl.pallas_call(functools.partial(kernel, n, m), out_shape=(jax.ShapeDtype...]
where the time goes in v7:
time: 48.9 us; the launch traced here: 48.7 us
  Pallas kernels  46.3 us (95%)
  between operations  2.4 us (5%)
    pallas_call x1, Pallas kernels, local(): pl.pallas_call(functools.partial(kernel, n, m), out_shape=(jax.ShapeDtype...  44.3 us
    pallas_call x1, Pallas kernels, local(): pl.pallas_call(functools.partial(leave_kernel, n), out_shape=jax.ShapeDty...  2.02 us

profile of v7, /device:TPU:1, one launch (start us, length us, event | category | flops | bytes accessed | tf_op | source)
XLA Modules:
  0.0 48.7 jit_solution(1095038409856799813)
XLA Ops:
  0.6 44.3 %shard_map.50 = (bf16[16,32,256]{2,1,0:T(8,128)(2,1)}, f32[1,1]{1,0:T(1,128)}) custom-call(s32[16]{0:T(128)} %counts.3, bf16[256,1024]{1,0:T(8,128)(2,1)} %t_ref.1, bf16[256,512]{1,0:T(8,128)(2,1)} %s_ref.1), custom_call_target="tpu_custom_call" | custom-call | tf_op jit(solution)/shard_map/pallas_call | solution.py:454
  44.9 2.0 %shard_map.51 = f32[256,512]{1,0:T(8,128)} custom-call(s32[16]{0:T(128)} %counts.3, bf16[16,32,256]{2,1,0:T(8,128)(2,1)} %get-tuple-element.4.g_ref), custom_call_target="tpu_custom_call" | custom-call | tf_op jit(solution)/shard_map/pallas_call | solution.py:482

commit v8 on v7

--- a/solution.py
+++ b/solution.py
@@ -335,8 +335,6 @@
     turned = turn(shift, TILE)
     s_load.wait()
     enter(s_own, turned, s_out)
-    t_load.wait()
-    enter(t_own, turned, t_out)
     start = jnp.int32(0)
     scalars = []
     for b in range(n):
@@ -348,6 +346,9 @@
 
     copies, keeps = [], []
     for kind, (src, dst) in enumerate(((s_out, s_in), (t_out, t_in))):
+        if kind:
+            t_load.wait()
+            enter(t_own, turned, t_out)
         for copy in copies[0] if kind else []:
             copy.wait_send()
         keeps.append(pltpu.make_async_copy(src.at[me], dst.at[me], own.at[kind]))

time: 48.9 us -> 48.9 us (level)
  no operation moved by 1% of the time
where the time goes in v8:
time: 48.9 us; the launch traced here: 48.7 us
  Pallas kernels  46.3 us (95%)
  between operations  2.4 us (5%)
    pallas_call x1, Pallas kernels, local(): pl.pallas_call(functools.partial(kernel, n, m), out_shape=(jax.ShapeDtype...  44.3 us
    pallas_call x1, Pallas kernels, local(): pl.pallas_call(functools.partial(leave_kernel, n), out_shape=jax.ShapeDty...  2.02 us

profile of v8, /device:TPU:1, one launch (start us, length us, event | category | flops | bytes accessed | tf_op | source)
XLA Modules:
  0.0 48.7 jit_solution(11197625160354658051)
XLA Ops:
  0.6 44.3 %shard_map.50 = (bf16[16,32,256]{2,1,0:T(8,128)(2,1)}, f32[1,1]{1,0:T(1,128)}) custom-call(s32[16]{0:T(128)} %counts.3, bf16[256,1024]{1,0:T(8,128)(2,1)} %t_ref.1, bf16[256,512]{1,0:T(8,128)(2,1)} %s_ref.1), custom_call_target="tpu_custom_call" | custom-call | tf_op jit(solution)/shard_map/pallas_call | solution.py:455
  44.9 2.0 %shard_map.51 = f32[256,512]{1,0:T(8,128)} custom-call(s32[16]{0:T(128)} %counts.3, bf16[16,32,256]{2,1,0:T(8,128)(2,1)} %get-tuple-element.4.g_ref), custom_call_target="tpu_custom_call" | custom-call | tf_op jit(solution)/shard_map/pallas_call | solution.py:483
